TPU v7x, 32 devices: a whole 2x2x4 slice. The times are simulated.
32 devices in a mesh: rep: 8 (over y, x, core), shard: 4 (over z).
Axes of the slice: x: 2, y: 2, z: 4, core: 2. Of those that a mesh axis runs over, the one named last changes fastest.
Arguments:
- inputs: bfloat16 [16, 1024, 1280], P('rep', 'shard'), may hold values from -6 to 6
- lengths: int32 [16], P('rep'), may hold values from 256 to 1024, as said below
- cotangent: bfloat16 [16, 1024, 1280], P('rep', 'shard'), may hold values from -6 to 6
- attn_gain: bfloat16 [2, 1280], P(None, 'shard'), may hold values from 0.5 to 1.5
- attn_shift: bfloat16 [2, 1280], P(None, 'shard'), may hold values from -1.25 to 1.25
- query_weight: bfloat16 [2, 1280, 1280], P(None, 'shard'), may hold values from -0.15625 to 0.15625
- query_bias: bfloat16 [2, 1280], P(None, 'shard'), may hold values from -1.25 to 1.25
- key_weight: bfloat16 [2, 1280, 1280], P(None, 'shard'), may hold values from -0.15625 to 0.15625
- value_weight: bfloat16 [2, 1280, 1280], P(None, 'shard'), may hold values from -0.15625 to 0.15625
- value_bias: bfloat16 [2, 1280], P(None, 'shard'), may hold values from -1.25 to 1.25
- out_weight: bfloat16 [2, 1280, 1280], P(None, 'shard'), may hold values from -2.5 to 2.5
- out_bias: bfloat16 [2, 1280], P(None, 'shard'), may hold values from -1.25 to 1.25
- mlp_gain: bfloat16 [2, 1280], P(None, 'shard'), may hold values from 0.5 to 1.5
- mlp_shift: bfloat16 [2, 1280], P(None, 'shard'), may hold values from -1.25 to 1.25
- up_weight: bfloat16 [2, 1280, 5120], P(None, 'shard'), may hold values from -0.15625 to 0.15625
- up_bias: bfloat16 [2, 5120], P(None, 'shard'), may hold values from -1.25 to 1.25
- down_weight: bfloat16 [2, 5120, 1280], P(None, 'shard'), may hold values from -0.078125 to 0.078125
- down_bias: bfloat16 [2, 1280], P(None, 'shard'), may hold values from -1.25 to 1.25
Outputs:
- output: bfloat16 [16, 1024, 1280], P('rep', 'shard')
- input_grad: float32 [16, 1024, 1280], P('rep', 'shard')
- attn_gain_grad: float32 [2, 1280], P(None, 'shard')
- attn_shift_grad: float32 [2, 1280], P(None, 'shard')
- query_weight_grad: float32 [2, 1280, 1280], P(None, 'shard')
- query_bias_grad: float32 [2, 1280], P(None, 'shard')
- key_weight_grad: float32 [2, 1280, 1280], P(None, 'shard')
- value_weight_grad: float32 [2, 1280, 1280], P(None, 'shard')
- value_bias_grad: float32 [2, 1280], P(None, 'shard')
- out_weight_grad: float32 [2, 1280, 1280], P(None, 'shard')
- out_bias_grad: float32 [2, 1280], P(None, 'shard')
- mlp_gain_grad: float32 [2, 1280], P(None, 'shard')
- mlp_shift_grad: float32 [2, 1280], P(None, 'shard')
- up_weight_grad: float32 [2, 1280, 5120], P(None, 'shard')
- up_bias_grad: float32 [2, 5120], P(None, 'shard')
- down_weight_grad: float32 [2, 5120, 1280], P(None, 'shard')
- down_bias_grad: float32 [2, 1280], P(None, 'shard')
Inputs may be any that keep to these rules, and one draw needn't show every extreme that they name: `lengths`: of the 2 clips on one index of rep, one (which, drawn from the seed) has all 1024 tokens valid.
All inputs are finite; a program needn't handle non-finite values.
Results may differ from a plain program's by a relative error of at most 0.02.
Values may be sent and summed in bfloat16 or wider, within the bound.
A program may use at most 576 MiB of HBM per device.

v0:
```python
import jax
import jax.numpy as jnp
from jax import lax
from jax.sharding import PartitionSpec as P

H = 16


EPSILON = 1e-05
NEGATIVE = -1e30


def norm_affine(values, norm_gain, norm_shift):
    center = values - jnp.mean(values, axis=-1, keepdims=True)
    spread = jnp.mean(center * center, axis=-1, keepdims=True)
    return center * lax.rsqrt(spread + EPSILON) * norm_gain + norm_shift


def gelu_exact(values):
    return jax.nn.gelu(values, approximate=False)


def project(left_operand, right_operand):
    return jnp.einsum(
        "csa,ab->csb", left_operand, right_operand, preferred_element_type=jnp.float32
    )


def project_back(left_operand, right_operand):
    return jnp.einsum(
        "csb,ab->csa", left_operand, right_operand, preferred_element_type=jnp.float32
    )


def weight_grad(left_operand, right_operand):
    return jnp.einsum(
        "csa,csb->ab", left_operand, right_operand, preferred_element_type=jnp.float32
    )


def column_sum(values):
    return jnp.sum(values.astype(jnp.float32), axis=(0, 1))


def layer_slice(params, layer_index):
    return tuple((weight_array[layer_index] for weight_array in params))


def fetch_forward(local_params):
    return (
        lax.all_gather(local_params[0], "shard", axis=0, tiled=True),
        lax.all_gather(local_params[1], "shard", axis=0, tiled=True),
        lax.all_gather(local_params[2], "shard", axis=0, tiled=True),
        lax.all_gather(local_params[3], "shard", axis=0, tiled=True),
        lax.all_gather(local_params[4], "shard", axis=0, tiled=True),
        lax.all_gather(local_params[5], "shard", axis=0, tiled=True),
        lax.all_gather(local_params[6], "shard", axis=0, tiled=True),
        lax.all_gather(local_params[7], "shard", axis=0, tiled=True),
        lax.all_gather(local_params[8], "shard", axis=0, tiled=True),
        lax.all_gather(local_params[9], "shard", axis=0, tiled=True),
        lax.all_gather(local_params[10], "shard", axis=0, tiled=True),
        lax.all_gather(local_params[11], "shard", axis=0, tiled=True),
        lax.all_gather(local_params[12], "shard", axis=0, tiled=True),
        lax.all_gather(local_params[13], "shard", axis=0, tiled=True),
        lax.all_gather(local_params[14], "shard", axis=0, tiled=True),
    )


def fetch_again(local_params):
    return (
        lax.all_gather(local_params[0], "shard", axis=0, tiled=True),
        lax.all_gather(local_params[1], "shard", axis=0, tiled=True),
        lax.all_gather(local_params[2], "shard", axis=0, tiled=True),
        lax.all_gather(local_params[3], "shard", axis=0, tiled=True),
        lax.all_gather(local_params[4], "shard", axis=0, tiled=True),
        lax.all_gather(local_params[5], "shard", axis=0, tiled=True),
        lax.all_gather(local_params[6], "shard", axis=0, tiled=True),
        lax.all_gather(local_params[7], "shard", axis=0, tiled=True),
        lax.all_gather(local_params[8], "shard", axis=0, tiled=True),
        lax.all_gather(local_params[9], "shard", axis=0, tiled=True),
        lax.all_gather(local_params[10], "shard", axis=0, tiled=True),
        lax.all_gather(local_params[11], "shard", axis=0, tiled=True),
        lax.all_gather(local_params[12], "shard", axis=0, tiled=True),
        lax.all_gather(local_params[13], "shard", axis=0, tiled=True),
        lax.all_gather(local_params[14], "shard", axis=0, tiled=True),
    )


def forward_layer(hidden_state, weights, lengths):
    (
        attn_gain,
        attn_shift,
        query_weight,
        query_bias,
        key_weight,
        value_weight,
        value_bias,
        out_weight,
        out_bias,
        mlp_gain,
        mlp_shift,
        up_weight,
        up_bias,
        down_weight,
        down_bias,
    ) = weights
    clip_count, row_count, model_width = hidden_state.shape
    head_size = model_width // H
    query_scale = float(head_size) ** (-0.5)
    normed = norm_affine(
        hidden_state, attn_gain.astype(jnp.float32), attn_shift.astype(jnp.float32)
    ).astype(jnp.bfloat16)
    query_low = (
        (project(normed, query_weight) + query_bias.astype(jnp.float32)) * query_scale
    ).astype(jnp.bfloat16)
    key_low = project(normed, key_weight).astype(jnp.bfloat16)
    value_low = (project(normed, value_weight) + value_bias.astype(jnp.float32)).astype(
        jnp.bfloat16
    )
    key_all, value_all = (
        lax.all_gather(key_low, "shard", axis=1, tiled=True),
        lax.all_gather(value_low, "shard", axis=1, tiled=True),
    )
    length_all = key_all.shape[1]
    valid_keys = jnp.arange(length_all, dtype=jnp.int32)[None, :] < lengths[:, None]
    query_heads = query_low.reshape(clip_count, row_count, H, head_size)
    key_heads = key_all.reshape(clip_count, length_all, H, head_size)
    value_heads = value_all.reshape(clip_count, length_all, H, head_size)
    scores = jnp.einsum(
        "cqhd,ckhd->chqk", query_heads, key_heads, preferred_element_type=jnp.float32
    )
    scores = jnp.where(valid_keys[:, None, None, :], scores, NEGATIVE)
    attention = jax.nn.softmax(scores, axis=-1)
    attention_low = attention.astype(jnp.bfloat16)
    context = jnp.einsum(
        "chqk,ckhd->cqhd", attention_low, value_heads, preferred_element_type=jnp.float32
    )
    context_low = context.reshape(clip_count, row_count, model_width).astype(jnp.bfloat16)
    middle = hidden_state + project(context_low, out_weight) + out_bias.astype(jnp.float32)
    hidden_in = norm_affine(
        middle, mlp_gain.astype(jnp.float32), mlp_shift.astype(jnp.float32)
    ).astype(jnp.bfloat16)
    pre_gelu = project(hidden_in, up_weight) + up_bias.astype(jnp.float32)
    active_low = gelu_exact(pre_gelu).astype(jnp.bfloat16)
    result = middle + project(active_low, down_weight) + down_bias.astype(jnp.float32)
    kept_values = (
        normed,
        query_heads,
        key_heads,
        value_heads,
        attention,
        attention_low,
        context_low,
        middle,
        hidden_in,
        pre_gelu,
        active_low,
    )
    return (result, kept_values)


def backward_layer(hidden_state, grad_after, weights, lengths):
    (
        attn_gain,
        attn_shift,
        query_weight,
        query_bias,
        key_weight,
        value_weight,
        value_bias,
        out_weight,
        out_bias,
        mlp_gain,
        mlp_shift,
        up_weight,
        up_bias,
        down_weight,
        down_bias,
    ) = weights
    unused, kept_values = forward_layer(hidden_state, weights, lengths)
    (
        normed,
        query_heads,
        key_heads,
        value_heads,
        attention,
        attention_low,
        context_low,
        middle,
        hidden_in,
        pre_gelu,
        active_low,
    ) = kept_values
    clip_count, row_count, model_width = hidden_state.shape
    length_all = key_heads.shape[1]
    head_size = model_width // H
    query_scale = float(head_size) ** (-0.5)
    grad_low = grad_after.astype(jnp.bfloat16)
    grad_active = project_back(grad_low, down_weight)
    unused, gelu_pull = jax.vjp(gelu_exact, pre_gelu)
    grad_pre = gelu_pull(grad_active)[0].astype(jnp.bfloat16)
    grad_hidden = project_back(grad_pre, up_weight)
    unused, mlp_pull = jax.vjp(
        norm_affine, middle, mlp_gain.astype(jnp.float32), mlp_shift.astype(jnp.float32)
    )
    grad_middle_norm, grad_mlp_gain, grad_mlp_shift = mlp_pull(grad_hidden)
    grad_middle = grad_after + grad_middle_norm
    middle_low = grad_middle.astype(jnp.bfloat16)
    grad_context = project_back(middle_low, out_weight).astype(jnp.bfloat16)
    grad_context = grad_context.reshape(clip_count, row_count, H, head_size)
    grad_attention = jnp.einsum(
        "cqhd,ckhd->chqk", grad_context, value_heads, preferred_element_type=jnp.float32
    )
    value_part = jnp.einsum(
        "chqk,cqhd->ckhd", attention_low, grad_context, preferred_element_type=jnp.float32
    )
    grad_scores = attention * (
        grad_attention - jnp.sum(attention * grad_attention, axis=-1, keepdims=True)
    )
    scores_low = grad_scores.astype(jnp.bfloat16)
    grad_query = jnp.einsum(
        "chqk,ckhd->cqhd", scores_low, key_heads, preferred_element_type=jnp.float32
    )
    grad_query = grad_query.reshape(clip_count, row_count, model_width).astype(jnp.bfloat16)
    key_part = jnp.einsum(
        "chqk,cqhd->ckhd", scores_low, query_heads, preferred_element_type=jnp.float32
    )
    key_summed, value_summed = (
        lax.psum_scatter(
            key_part.reshape(clip_count, length_all, model_width).astype(jnp.bfloat16),
            "shard",
            scatter_dimension=1,
            tiled=True,
        ).astype(jnp.float32),
        lax.psum_scatter(
            value_part.reshape(clip_count, length_all, model_width).astype(jnp.bfloat16),
            "shard",
            scatter_dimension=1,
            tiled=True,
        ).astype(jnp.float32),
    )
    key_grad_low = key_summed.astype(jnp.bfloat16)
    value_grad_low = value_summed.astype(jnp.bfloat16)
    grad_normed = (
        project_back(grad_query, query_weight) * query_scale
        + project_back(key_grad_low, key_weight)
        + project_back(value_grad_low, value_weight)
    )
    unused, attn_pull = jax.vjp(
        norm_affine, hidden_state, attn_gain.astype(jnp.float32), attn_shift.astype(jnp.float32)
    )
    grad_input_norm, grad_attn_gain, grad_attn_shift = attn_pull(grad_normed)
    grad_before = grad_middle + grad_input_norm
    grad_down = weight_grad(active_low, grad_low)
    grad_down_bias = column_sum(grad_low)
    grad_up = weight_grad(hidden_in, grad_pre)
    grad_up_bias = column_sum(grad_pre)
    grad_out_weight = weight_grad(context_low, middle_low)
    grad_out_bias = column_sum(middle_low)
    grad_query_weight = weight_grad(normed, grad_query) * query_scale
    grad_query_bias = column_sum(grad_query) * query_scale
    grad_key_weight = weight_grad(normed, key_grad_low)
    grad_value_weight = weight_grad(normed, value_grad_low)
    grad_value_bias = column_sum(value_grad_low)
    owned_grads = (
        lax.psum_scatter(
            grad_attn_gain.astype(jnp.bfloat16), "shard", scatter_dimension=0, tiled=True
        ).astype(jnp.float32),
        lax.psum_scatter(
            grad_attn_shift.astype(jnp.bfloat16), "shard", scatter_dimension=0, tiled=True
        ).astype(jnp.float32),
        lax.psum_scatter(
            grad_query_weight.astype(jnp.bfloat16), "shard", scatter_dimension=0, tiled=True
        ).astype(jnp.float32),
        lax.psum_scatter(
            grad_query_bias.astype(jnp.bfloat16), "shard", scatter_dimension=0, tiled=True
        ).astype(jnp.float32),
        lax.psum_scatter(
            grad_key_weight.astype(jnp.bfloat16), "shard", scatter_dimension=0, tiled=True
        ).astype(jnp.float32),
        lax.psum_scatter(
            grad_value_weight.astype(jnp.bfloat16), "shard", scatter_dimension=0, tiled=True
        ).astype(jnp.float32),
        lax.psum_scatter(
            grad_value_bias.astype(jnp.bfloat16), "shard", scatter_dimension=0, tiled=True
        ).astype(jnp.float32),
        lax.psum_scatter(
            grad_out_weight.astype(jnp.bfloat16), "shard", scatter_dimension=0, tiled=True
        ).astype(jnp.float32),
        lax.psum_scatter(
            grad_out_bias.astype(jnp.bfloat16), "shard", scatter_dimension=0, tiled=True
        ).astype(jnp.float32),
        lax.psum_scatter(
            grad_mlp_gain.astype(jnp.bfloat16), "shard", scatter_dimension=0, tiled=True
        ).astype(jnp.float32),
        lax.psum_scatter(
            grad_mlp_shift.astype(jnp.bfloat16), "shard", scatter_dimension=0, tiled=True
        ).astype(jnp.float32),
        lax.psum_scatter(
            grad_up.astype(jnp.bfloat16), "shard", scatter_dimension=0, tiled=True
        ).astype(jnp.float32),
        lax.psum_scatter(
            grad_up_bias.astype(jnp.bfloat16), "shard", scatter_dimension=0, tiled=True
        ).astype(jnp.float32),
        lax.psum_scatter(
            grad_down.astype(jnp.bfloat16), "shard", scatter_dimension=0, tiled=True
        ).astype(jnp.float32),
        lax.psum_scatter(
            grad_down_bias.astype(jnp.bfloat16), "shard", scatter_dimension=0, tiled=True
        ).astype(jnp.float32),
    )
    return (grad_before, owned_grads)


def replica_layer(owned_grads):
    return (
        lax.psum(owned_grads[0].astype(jnp.bfloat16), "rep").astype(jnp.float32),
        lax.psum(owned_grads[1].astype(jnp.bfloat16), "rep").astype(jnp.float32),
        lax.psum(owned_grads[2].astype(jnp.bfloat16), "rep").astype(jnp.float32),
        lax.psum(owned_grads[3].astype(jnp.bfloat16), "rep").astype(jnp.float32),
        lax.psum(owned_grads[4].astype(jnp.bfloat16), "rep").astype(jnp.float32),
        lax.psum(owned_grads[5].astype(jnp.bfloat16), "rep").astype(jnp.float32),
        lax.psum(owned_grads[6].astype(jnp.bfloat16), "rep").astype(jnp.float32),
        lax.psum(owned_grads[7].astype(jnp.bfloat16), "rep").astype(jnp.float32),
        lax.psum(owned_grads[8].astype(jnp.bfloat16), "rep").astype(jnp.float32),
        lax.psum(owned_grads[9].astype(jnp.bfloat16), "rep").astype(jnp.float32),
        lax.psum(owned_grads[10].astype(jnp.bfloat16), "rep").astype(jnp.float32),
        lax.psum(owned_grads[11].astype(jnp.bfloat16), "rep").astype(jnp.float32),
        lax.psum(owned_grads[12].astype(jnp.bfloat16), "rep").astype(jnp.float32),
        lax.psum(owned_grads[13].astype(jnp.bfloat16), "rep").astype(jnp.float32),
        lax.psum(owned_grads[14].astype(jnp.bfloat16), "rep").astype(jnp.float32),
    )


def shards(
    inputs,
    lengths,
    cotangent,
    attn_gain,
    attn_shift,
    query_weight,
    query_bias,
    key_weight,
    value_weight,
    value_bias,
    out_weight,
    out_bias,
    mlp_gain,
    mlp_shift,
    up_weight,
    up_bias,
    down_weight,
    down_bias,
):
    params = (
        attn_gain,
        attn_shift,
        query_weight,
        query_bias,
        key_weight,
        value_weight,
        value_bias,
        out_weight,
        out_bias,
        mlp_gain,
        mlp_shift,
        up_weight,
        up_bias,
        down_weight,
        down_bias,
    )
    layers = attn_gain.shape[0]
    hidden_state = inputs.astype(jnp.float32)
    kept_inputs = []
    kept_weights = []
    for layer_index in range(layers):
        gathered = fetch_forward(layer_slice(params, layer_index))
        kept_inputs.append(hidden_state)
        kept_weights.append(gathered)
        hidden_state, unused = forward_layer(hidden_state, gathered, lengths)
    output = hidden_state.astype(jnp.bfloat16)
    row_count = inputs.shape[1]
    first_row = lax.axis_index("shard") * row_count
    positions = first_row + jnp.arange(row_count, dtype=jnp.int32)
    row_mask = (positions[None, :] < lengths[:, None]).astype(jnp.float32)
    grad_state = cotangent.astype(jnp.float32) * row_mask[:, :, None]
    owned_list = [None] * layers
    for layer_index in reversed(range(layers)):
        gathered = fetch_again(layer_slice(params, layer_index))
        grad_state, owned_grads = backward_layer(
            kept_inputs[layer_index], grad_state, gathered, lengths
        )
        owned_grads = replica_layer(owned_grads)
        owned_list[layer_index] = owned_grads
    stacked = tuple(
        (
            jnp.stack([owned_list[layer_index][member] for layer_index in range(layers)])
            for member in range(15)
        )
    )
    return (
        output,
        grad_state,
        stacked[0],
        stacked[1],
        stacked[2],
        stacked[3],
        stacked[4],
        stacked[5],
        stacked[6],
        stacked[7],
        stacked[8],
        stacked[9],
        stacked[10],
        stacked[11],
        stacked[12],
        stacked[13],
        stacked[14],
    )


def solution(mesh):
    placed = (
        P("rep", "shard", None),
        P("rep"),
        P("rep", "shard", None),
        P(None, "shard"),
        P(None, "shard"),
        P(None, "shard", None),
        P(None, "shard"),
        P(None, "shard", None),
        P(None, "shard", None),
        P(None, "shard"),
        P(None, "shard", None),
        P(None, "shard"),
        P(None, "shard"),
        P(None, "shard"),
        P(None, "shard", None),
        P(None, "shard"),
        P(None, "shard", None),
        P(None, "shard"),
    )
    return jax.shard_map(
        shards,
        mesh=mesh,
        in_specs=placed,
        out_specs=(
            P("rep", "shard", None),
            P("rep", "shard", None),
            P(None, "shard"),
            P(None, "shard"),
            P(None, "shard", None),
            P(None, "shard"),
            P(None, "shard", None),
            P(None, "shard", None),
            P(None, "shard"),
            P(None, "shard", None),
            P(None, "shard"),
            P(None, "shard"),
            P(None, "shard"),
            P(None, "shard", None),
            P(None, "shard"),
            P(None, "shard", None),
            P(None, "shard"),
        ),
        check_vma=False,
    )
```

profile of v0, /device:TPU:11, one launch (start us, length us, event | category | flops | bytes accessed | tf_op | source)
XLA Modules:
  0.0 4076.6 jit_solution(18159239028610461812)
XLA Ops:
  33.2 16.7 all-reduce.37
  50.7 25.9 all-gather.59.cloned.1.call-done
  81.8 61.4 %all-gather.55.cloned.1.call-done = bf16[1,1280,1280]{2,1,0:T(8,128)(2,1)} async-done(((bf16[1,320,1280]{2,1,0:T(8,128)(2,1)}), bf16[1,1280,1280]{2,1,0:T(8,128)(2,1)}) %all-gather.55.cloned.1.call-update) | async-done | bytes 3276816 | tf_op jit(solution)/shard_map/all_gather | solution.py:56
  164.5 10.6 all-gather.12
  175.1 34.8 all-gather.57.cloned.1.call-done
  216.8 91.6 %all-gather.49.cloned.1.call-done = bf16[2,1024,1280]{2,1,0:T(8,128)(2,1)} async-done(((bf16[2,256,1280]{2,1,0:T(8,128)(2,1)}), bf16[2,1024,1280]{2,1,0:T(8,128)(2,1)}) %all-gather.49.cloned.1.call-update) | async-done | bytes 5242896 | tf_op jit(solution)/shard_map/all_gather | solution.py:121
  316.4 17.7 fusion.204
  334.1 72.8 %all-gather.47.cloned.1.call-done = bf16[2,1024,1280]{2,1,0:T(8,128)(2,1)} async-done(((bf16[2,256,1280]{2,1,0:T(8,128)(2,1)}), bf16[2,1024,1280]{2,1,0:T(8,128)(2,1)}) %all-gather.47.cloned.1.call-update) | async-done | bytes 5242896 | tf_op jit(solution)/shard_map/all_gather | solution.py:122
  414.8 15.7 fusion.159
  430.6 42.6 %all-gather.61.cloned.1.call-done = bf16[1,1280,1280]{2,1,0:T(8,128)(2,1)} async-done(((bf16[1,320,1280]{2,1,0:T(8,128)(2,1)}), bf16[1,1280,1280]{2,1,0:T(8,128)(2,1)}) %all-gather.61.cloned.1.call-update) | async-done | bytes 3276816 | tf_op jit(solution)/shard_map/all_gather | solution.py:58
  479.2 221.2 %all-gather.63.cloned.1.call-done = bf16[1,1280,5120]{2,1,0:T(8,128)(2,1)} async-done(((bf16[1,320,5120]{2,1,0:T(8,128)(2,1)}), bf16[1,1280,5120]{2,1,0:T(8,128)(2,1)}) %all-gather.63.cloned.1.call-update) | async-done | bytes 13107216 | tf_op jit(solution)/shard_map/all_gather | solution.py:62
  700.4 29.2 fusion.157
  729.7 26.7 multiply_convert_fusion.3
  756.4 171.1 %all-gather.65.cloned.1.call-done = bf16[1,5120,1280]{2,1,0:T(8,128)(2,1)} async-done(((bf16[1,1280,1280]{2,1,0:T(8,128)(2,1)}), bf16[1,5120,1280]{2,1,0:T(8,128)(2,1)}) %all-gather.65.cloned.1.call-update) | async-done | bytes 13107216 | tf_op jit(solution)/shard_map/all_gather | solution.py:64
  927.6 13.2 fusion.206
  943.8 49.6 %all-gather.67.cloned.1.call-done = bf16[1,1280,1280]{2,1,0:T(8,128)(2,1)} async-done(((bf16[1,320,1280]{2,1,0:T(8,128)(2,1)}), bf16[1,1280,1280]{2,1,0:T(8,128)(2,1)}) %all-gather.67.cloned.1.call-update) | async-done | bytes 3276816 | tf_op jit(solution)/shard_map/all_gather | solution.py:56
  998.7 60.4 %all-gather.71.cloned.1.call-done = bf16[1,1280,1280]{2,1,0:T(8,128)(2,1)} async-done(((bf16[1,320,1280]{2,1,0:T(8,128)(2,1)}), bf16[1,1280,1280]{2,1,0:T(8,128)(2,1)}) %all-gather.71.cloned.1.call-update) | async-done | bytes 3276816 | tf_op jit(solution)/shard_map/all_gather | solution.py:55
  1077.0 48.3 %all-gather.69.cloned.1.call-done = bf16[1,1280,1280]{2,1,0:T(8,128)(2,1)} async-done(((bf16[1,320,1280]{2,1,0:T(8,128)(2,1)}), bf16[1,1280,1280]{2,1,0:T(8,128)(2,1)}) %all-gather.69.cloned.1.call-update) | async-done | bytes 3276816 | tf_op jit(solution)/shard_map/all_gather | solution.py:53
  1133.4 90.4 %all-gather.51.cloned.1.call-done = bf16[2,1024,1280]{2,1,0:T(8,128)(2,1)} async-done(((bf16[2,256,1280]{2,1,0:T(8,128)(2,1)}), bf16[2,1024,1280]{2,1,0:T(8,128)(2,1)}) %all-gather.51.cloned.1.call-update) | async-done | bytes 5242896 | tf_op jit(solution)/shard_map/all_gather | solution.py:122
  1231.6 90.1 %all-gather.53.cloned.1.call-done = bf16[2,1024,1280]{2,1,0:T(8,128)(2,1)} async-done(((bf16[2,256,1280]{2,1,0:T(8,128)(2,1)}), bf16[2,1024,1280]{2,1,0:T(8,128)(2,1)}) %all-gather.53.cloned.1.call-update) | async-done | bytes 5242896 | tf_op jit(solution)/shard_map/all_gather | solution.py:121
  1329.7 18.0 fusion.207
  1347.7 16.1 fusion.162
  1363.8 23.7 all-gather.73.cloned.1.call-done
  1393.9 220.6 %all-gather.75.cloned.1.call-done = bf16[1,1280,5120]{2,1,0:T(8,128)(2,1)} async-done(((bf16[1,320,5120]{2,1,0:T(8,128)(2,1)}), bf16[1,1280,5120]{2,1,0:T(8,128)(2,1)}) %all-gather.75.cloned.1.call-update) | async-done | bytes 13107216 | tf_op jit(solution)/shard_map/all_gather | solution.py:62
  1614.5 17.1 fusion.158
  1631.6 26.8 multiply_convert_fusion.2
  1658.4 183.1 %all-gather.77.cloned.1.call-done = bf16[1,5120,1280]{2,1,0:T(8,128)(2,1)} async-done(((bf16[1,1280,1280]{2,1,0:T(8,128)(2,1)}), bf16[1,5120,1280]{2,1,0:T(8,128)(2,1)}) %all-gather.77.cloned.1.call-update) | async-done | bytes 13107216 | tf_op jit(solution)/shard_map/all_gather | solution.py:64
  1841.6 20.2 fusion.209
  1861.8 15.2 multiply_reduce_fusion.2
  1886.0 14.7 fusion.117
  1908.7 23.6 multiply_reduce_fusion.1
  1932.3 28.0 multiply_convert_fusion.1
  1960.2 11.1 convolution_convert_fusion.1
  1979.3 12.8 convert_reduce_fusion.1
  1992.0 11.5 reduce-scatter.19.cloned.1.call-done
  2008.2 91.7 %reduce-scatter.17.cloned.1.call-done = bf16[2,256,1280]{2,1,0:T(8,128)(2,1)} async-done(((bf16[2,1024,1280]{2,1,0:T(8,128)(2,1)}), bf16[2,256,1280]{2,1,0:T(8,128)(2,1)}) %reduce-scatter.17.cloned.1.call-update) | async-done | bytes 1310736 | tf_op jit(solution)/shard_map/reduce_scatter | solution.py:229
  2112.7 20.8 fusion.210
  2133.6 15.0 multiply_reduce_fusion.3
  2157.1 14.7 fusion.114
  2179.8 23.7 multiply_reduce_fusion
  2203.5 27.9 multiply_convert_fusion
  2231.4 11.2 convolution_convert_fusion
  2277.5 11.4 convert_reduce_fusion.2
  2294.6 12.9 bitcast_convert_fusion.2
  2308.9 14.0 bitcast_convert_fusion
  2328.1 42.5 %reduce-scatter.21.cloned.1.call-done = bf16[2,256,1280]{2,1,0:T(8,128)(2,1)} async-done(((bf16[2,1024,1280]{2,1,0:T(8,128)(2,1)}), bf16[2,256,1280]{2,1,0:T(8,128)(2,1)}) %reduce-scatter.21.cloned.1.call-update) | async-done | bytes 1310736 | tf_op jit(solution)/shard_map/reduce_scatter | solution.py:229
  2376.4 12.9 bitcast_convert_fusion.3
  2389.4 12.5 bitcast_convert_fusion.1
  2402.3 33.1 reduce-scatter.39.cloned.1.call-done
  2435.3 65.3 %reduce-scatter.27.cloned.1.call-done = bf16[320,1280]{1,0:T(8,128)(2,1)} async-done(((bf16[1280,1280]{1,0:T(8,128)(2,1)}), bf16[320,1280]{1,0:T(8,128)(2,1)}) %reduce-scatter.27.cloned.1.call-update) | async-done | bytes 819216 | tf_op jit(solution)/shard_map/reduce_scatter | solution.py:272
  2500.7 64.8 %reduce-scatter.35.cloned.1.call-done = bf16[320,1280]{1,0:T(8,128)(2,1)} async-done(((bf16[1280,1280]{1,0:T(8,128)(2,1)}), bf16[320,1280]{1,0:T(8,128)(2,1)}) %reduce-scatter.35.cloned.1.call-update) | async-done | bytes 819216 | tf_op jit(solution)/shard_map/reduce_scatter | solution.py:281
  2565.4 64.6 %reduce-scatter.37.cloned.1.call-done = bf16[320,1280]{1,0:T(8,128)(2,1)} async-done(((bf16[1280,1280]{1,0:T(8,128)(2,1)}), bf16[320,1280]{1,0:T(8,128)(2,1)}) %reduce-scatter.37.cloned.1.call-update) | async-done | bytes 819216 | tf_op jit(solution)/shard_map/reduce_scatter | solution.py:287
  2630.0 65.3 %reduce-scatter.31.cloned.1.call-done = bf16[320,1280]{1,0:T(8,128)(2,1)} async-done(((bf16[1280,1280]{1,0:T(8,128)(2,1)}), bf16[320,1280]{1,0:T(8,128)(2,1)}) %reduce-scatter.31.cloned.1.call-update) | async-done | bytes 819216 | tf_op jit(solution)/shard_map/reduce_scatter | solution.py:278
  2695.4 65.2 %reduce-scatter.25.cloned.1.call-done = bf16[320,1280]{1,0:T(8,128)(2,1)} async-done(((bf16[1280,1280]{1,0:T(8,128)(2,1)}), bf16[320,1280]{1,0:T(8,128)(2,1)}) %reduce-scatter.25.cloned.1.call-update) | async-done | bytes 819216 | tf_op jit(solution)/shard_map/reduce_scatter | solution.py:272
  2760.5 223.6 %reduce-scatter.43.cloned.1.call-done = bf16[320,5120]{1,0:T(8,128)(2,1)} async-done(((bf16[1280,5120]{1,0:T(8,128)(2,1)}), bf16[320,5120]{1,0:T(8,128)(2,1)}) %reduce-scatter.43.cloned.1.call-update) | async-done | bytes 3276816 | tf_op jit(solution)/shard_map/reduce_scatter | solution.py:299
  2984.2 223.7 %reduce-scatter.47.cloned.1.call-done = bf16[1280,1280]{1,0:T(8,128)(2,1)} async-done(((bf16[5120,1280]{1,0:T(8,128)(2,1)}), bf16[1280,1280]{1,0:T(8,128)(2,1)}) %reduce-scatter.47.cloned.1.call-update) | async-done | bytes 3276816 | tf_op jit(solution)/shard_map/reduce_scatter | solution.py:305
  3207.9 65.3 %reduce-scatter.33.cloned.1.call-done = bf16[320,1280]{1,0:T(8,128)(2,1)} async-done(((bf16[1280,1280]{1,0:T(8,128)(2,1)}), bf16[320,1280]{1,0:T(8,128)(2,1)}) %reduce-scatter.33.cloned.1.call-update) | async-done | bytes 819216 | tf_op jit(solution)/shard_map/reduce_scatter | solution.py:281
  3273.2 65.2 %reduce-scatter.29.cloned.1.call-done = bf16[320,1280]{1,0:T(8,128)(2,1)} async-done(((bf16[1280,1280]{1,0:T(8,128)(2,1)}), bf16[320,1280]{1,0:T(8,128)(2,1)}) %reduce-scatter.29.cloned.1.call-update) | async-done | bytes 819216 | tf_op jit(solution)/shard_map/reduce_scatter | solution.py:278
  3338.4 223.8 %reduce-scatter.41.cloned.1.call-done = bf16[320,5120]{1,0:T(8,128)(2,1)} async-done(((bf16[1280,5120]{1,0:T(8,128)(2,1)}), bf16[320,5120]{1,0:T(8,128)(2,1)}) %reduce-scatter.41.cloned.1.call-update) | async-done | bytes 3276816 | tf_op jit(solution)/shard_map/reduce_scatter | solution.py:299
  3562.2 223.7 %reduce-scatter.45.cloned.1.call-done = bf16[1280,1280]{1,0:T(8,128)(2,1)} async-done(((bf16[5120,1280]{1,0:T(8,128)(2,1)}), bf16[1280,1280]{1,0:T(8,128)(2,1)}) %reduce-scatter.45.cloned.1.call-update) | async-done | bytes 3276816 | tf_op jit(solution)/shard_map/reduce_scatter | solution.py:305
  3801.8 14.3 all-reduce.36
  3817.7 26.9 all-reduce.34
  3853.2 14.6 fusion.120
  3867.8 180.3 %all-reduce.40.cloned.1.call-done = (bf16[1,320,1280]{2,1,0:T(8,128)(2,1)}, bf16[1,320,1280]{2,1,0:T(8,128)(2,1)}, bf16[1,320,1280]{2,1,0:T(8,128)(2,1)}, bf16[1...) async-done(((bf16[1,320,1280]{2,1,0:T(8,128)(2,1)}, ...) | async-done | bytes 19660816 | tf_op jit(solution)/shard_map/psum | solution.py:319
  (514 shorter events, 294.4 us)
Async XLA Ops:
  7.2 69.5 %all-gather.59.cloned.1.call-start = ((), (), s32[]{:S(2)}) async-start(), calls=%async_computation.38 | async-start | bytes 4096000 | tf_op jit(solution)/shard_map/all_gather | solution.py:55
  10.0 133.1 %all-gather.55.cloned.1.call-start = ((), (), s32[]{:S(2)}) async-start(), calls=%async_computation.36 | async-start | bytes 4096000 | tf_op jit(solution)/shard_map/all_gather | solution.py:56
  11.4 38.5 copy-start.2
  11.5 198.4 %all-gather.57.cloned.1.call-start = ((), (), s32[]{:S(2)}) async-start(), calls=%async_computation.37 | async-start | bytes 4096000 | tf_op jit(solution)/shard_map/all_gather | solution.py:53
  13.3 295.1 %all-gather.49.cloned.1.call-start = ((), (), s32[]{:S(2)}) async-start(), calls=%async_computation.17 | async-start | bytes 6553600 | tf_op jit(solution)/shard_map/all_gather | solution.py:121
  49.9 160.0 %copy-start.56 = (f32[1280]{0:T(1024)}, f32[1280]{0:T(1024)S(1)}, u32[]{:S(2)}) copy-start(f32[1280]{0:T(1024)S(1)} %convert_element_type.564) | copy-start | bytes 15364
  49.9 160.0 %copy-start.99 = (f32[1280]{0:T(1024)}, f32[1280]{0:T(1024)S(1)}, u32[]{:S(2)}) copy-start(f32[1280]{0:T(1024)S(1)} %convert_element_type.565) | copy-start | bytes 15364
  50.2 159.7 %copy-start.60 = (f32[2,256]{1,0:T(2,128)}, f32[2,256]{1,0:T(2,128)S(1)}, u32[]{:S(2)}) copy-start(f32[2,256]{1,0:T(2,128)S(1)} %broadcast_multiply_fusion.3) | copy-start | bytes 6148
  50.7 31.0 copy-start.80
  50.7 159.2 %copy-start.74 = (f32[2,256]{1,0:T(2,128)}, f32[2,256]{1,0:T(2,128)S(1)}, u32[]{:S(2)}) copy-start(f32[2,256]{1,0:T(2,128)S(1)} %fusion.172) | copy-start | bytes 6148
  81.7 325.2 %all-gather.47.cloned.1.call-start = ((), (), s32[]{:S(2)}) async-start(), calls=%async_computation.16 | async-start | bytes 6553600 | tf_op jit(solution)/shard_map/all_gather | solution.py:122
  81.8 66.5 %copy-start.34 = (bf16[2,320,1280]{2,1,0:T(8,128)(2,1)S(1)}, bf16[2,320,1280]{2,1,0:T(8,128)(2,1)}, u32[]{:S(2)}) copy-start(bf16[2,320,1280]{2,1,0:T(8,128)(2,1)} %param.28) | copy-start | bytes 4915204
  148.2 325.0 %all-gather.61.cloned.1.call-start = ((), (), s32[]{:S(2)}) async-start(), calls=%async_computation.39 | async-start | bytes 4096000 | tf_op jit(solution)/shard_map/all_gather | solution.py:58
  149.6 550.8 %all-gather.63.cloned.1.call-start = ((), (), s32[]{:S(2)}) async-start(), calls=%async_computation.40 | async-start | bytes 16384000 | tf_op jit(solution)/shard_map/all_gather | solution.py:62
  155.8 771.8 %all-gather.65.cloned.1.call-start = ((), (), s32[]{:S(2)}) async-start(), calls=%async_computation.41 | async-start | bytes 16384000 | tf_op jit(solution)/shard_map/all_gather | solution.py:64
  162.2 831.2 %all-gather.67.cloned.1.call-start = ((), (), s32[]{:S(2)}) async-start(), calls=%async_computation.42 | async-start | bytes 4096000 | tf_op jit(solution)/shard_map/all_gather | solution.py:56
  162.9 896.2 %all-gather.71.cloned.1.call-start = ((), (), s32[]{:S(2)}) async-start(), calls=%async_computation.44 | async-start | bytes 4096000 | tf_op jit(solution)/shard_map/all_gather | solution.py:55
  163.5 961.8 %all-gather.69.cloned.1.call-start = ((), (), s32[]{:S(2)}) async-start(), calls=%async_computation.43 | async-start | bytes 4096000 | tf_op jit(solution)/shard_map/all_gather | solution.py:53
  164.2 1059.5 %all-gather.51.cloned.1.call-start = ((), (), s32[]{:S(2)}) async-start(), calls=%async_computation.18 | async-start | bytes 6553600 | tf_op jit(solution)/shard_map/all_gather | solution.py:122
  164.4 536.0 %copy-start.64 = (f32[1280]{0:T(1024)}, f32[1280]{0:T(1024)S(1)}, u32[]{:S(2)}) copy-start(f32[1280]{0:T(1024)S(1)} %convert_element_type.569) | copy-start | bytes 15364
  164.4 776.9 %copy-start.50 = (f32[1280]{0:T(1024)}, f32[1280]{0:T(1024)S(1)}, u32[]{:S(2)}) copy-start(f32[1280]{0:T(1024)S(1)} %convert_element_type.572) | copy-start | bytes 15364
  164.4 536.0 %copy-start.101 = (f32[1280]{0:T(1024)}, f32[1280]{0:T(1024)S(1)}, u32[]{:S(2)}) copy-start(f32[1280]{0:T(1024)S(1)} %convert_element_type.570) | copy-start | bytes 15364
  175.1 554.5 %copy-start.54 = (f32[1,5120]{1,0:T(1,128)}, f32[1,5120]{1,0:T(1,128)S(1)}, u32[]{:S(2)}) copy-start(f32[1,5120]{1,0:T(1,128)S(1)} %convert_element_type.553) | copy-start | bytes 61444
  216.8 99.6 %copy-start.16 = (bf16[2,256,1280]{1,2,0:T(8,128)(2,1)}, bf16[2,256,1280]{1,2,0:T(8,128)(2,1)S(1)}, u32[]{:S(2)}) copy-start(bf16[2,256,1280]{1,2,0:T(8,128)(2,1)S(1)} %copy.100) | copy-start | bytes 3932164
  334.1 80.7 %copy-start.58 = (f32[2,16,256]{2,1,0:T(8,128)}, f32[2,16,256]{2,1,0:T(8,128)S(1)}, u32[]{:S(2)}) copy-start(f32[2,16,256]{2,1,0:T(8,128)S(1)} %get-tuple-element.146) | copy-start | bytes 98308
  430.6 46.7 %copy-start.30 = (bf16[2,16,80,256]{3,2,1,0:T(8,128)(2,1)}, bf16[2,16,80,256]{3,2,1,0:T(8,128)(2,1)S(1)}, u32[]{:S(2)}) copy-start(bf16[2,16,80,256]{3,2,1,0:T(8,128)(2,1)S(1)} %fusion.159) | copy-start | bytes 3932164
  477.3 252.3 %copy-start.86 = (f32[2,256]{1,0:T(2,128)}, f32[2,256]{1,0:T(2,128)S(1)}, u32[]{:S(2)}) copy-start(f32[2,256]{1,0:T(2,128)S(1)} %broadcast_multiply_fusion.2) | copy-start | bytes 6148
  479.2 250.5 %copy-start.82 = (f32[2,256]{1,0:T(2,128)}, f32[2,256]{1,0:T(2,128)S(1)}, u32[]{:S(2)}) copy-start(f32[2,256]{1,0:T(2,128)S(1)} %multiply_reduce_fusion.10) | copy-start | bytes 6148
  479.2 250.5 %copy-start.105 = (f32[2,256]{1,0:T(2,128)}, f32[2,256]{1,0:T(2,128)S(1)}, u32[]{:S(2)}) copy-start(f32[2,256]{1,0:T(2,128)S(1)} %fusion.173) | copy-start | bytes 6148
  940.8 446.7 %copy-start = (f32[2,256,1280]{2,1,0:T(8,128)}, f32[2,256,1280]{2,1,0:T(8,128)S(1)}, u32[]{:S(2)}) copy-start(f32[2,256,1280]{2,1,0:T(8,128)S(1)} %get-tuple-element.152) | copy-start | bytes 7864324
  941.2 57.4 %copy-start.84 = (f32[2,256]{1,0:T(2,128)}, f32[2,256]{1,0:T(2,128)S(1)}, u32[]{:S(2)}) copy-start(f32[2,256]{1,0:T(2,128)S(1)} %multiply_reduce_fusion.9) | copy-start | bytes 6148
  998.6 323.1 %all-gather.53.cloned.1.call-start = ((), (), s32[]{:S(2)}) async-start(), calls=%async_computation.19 | async-start | bytes 6553600 | tf_op jit(solution)/shard_map/all_gather | solution.py:121
  1064.4 323.1 %all-gather.73.cloned.1.call-start = ((), (), s32[]{:S(2)}) async-start(), calls=%async_computation.45 | async-start | bytes 4096000 | tf_op jit(solution)/shard_map/all_gather | solution.py:58
  1065.0 549.5 %all-gather.75.cloned.1.call-start = ((), (), s32[]{:S(2)}) async-start(), calls=%async_computation.46 | async-start | bytes 16384000 | tf_op jit(solution)/shard_map/all_gather | solution.py:62
  1065.6 776.0 %all-gather.77.cloned.1.call-start = ((), (), s32[]{:S(2)}) async-start(), calls=%async_computation.47 | async-start | bytes 16384000 | tf_op jit(solution)/shard_map/all_gather | solution.py:64
  1066.2 937.4 %reduce-scatter.19.cloned.1.call-start = ((), (), s32[]{:S(2)}) async-start(), calls=%async_computation.21 | async-start | bytes 6553600 | tf_op jit(solution)/shard_map/reduce_scatter | solution.py:235
  1066.2 810.8 %copy-start.67 = (f32[1280]{0:T(1024)}, f32[1280]{0:T(1024)S(1)}, u32[]{:S(2)}) copy-start(f32[1280]{0:T(1024)S(1)} %convert_element_type.577) | copy-start | bytes 15364
  1066.2 548.3 %copy-start.103 = (f32[1280]{0:T(1024)}, f32[1280]{0:T(1024)S(1)}, u32[]{:S(2)}) copy-start(f32[1280]{0:T(1024)S(1)} %convert_element_type.578) | copy-start | bytes 15364
  1077.0 802.8 %copy-start.71 = (f32[2,256]{1,0:T(2,128)}, f32[2,256]{1,0:T(2,128)S(1)}, u32[]{:S(2)}) copy-start(f32[2,256]{1,0:T(2,128)S(1)} %compare_convert_fusion) | copy-start | bytes 6148
  1392.0 485.1 %copy-start.89 = (f32[2,256]{1,0:T(2,128)}, f32[2,256]{1,0:T(2,128)S(1)}, u32[]{:S(2)}) copy-start(f32[2,256]{1,0:T(2,128)S(1)} %broadcast_multiply_fusion) | copy-start | bytes 6148
  1393.9 483.1 %copy-start.108 = (f32[2,256]{1,0:T(2,128)}, f32[2,256]{1,0:T(2,128)S(1)}, u32[]{:S(2)}) copy-start(f32[2,256]{1,0:T(2,128)S(1)} %fusion.175) | copy-start | bytes 6148
  1908.6 191.4 %reduce-scatter.17.cloned.1.call-start = ((), (), s32[]{:S(2)}) async-start(), calls=%async_computation.20 | async-start | bytes 6553600 | tf_op jit(solution)/shard_map/reduce_scatter | solution.py:229
  1932.3 28.0 copy-start.18
  1979.2 24.3 copy-start.127
  1979.2 343.7 %reduce-scatter.23.cloned.1.call-start = ((), (), s32[]{:S(2)}) async-start(), calls=%async_computation.23 | async-start | bytes 6553600 | tf_op jit(solution)/shard_map/reduce_scatter | solution.py:235
  2008.2 96.1 %copy-start.1 = (f32[2,256,1280]{2,1,0:T(8,128)S(1)}, f32[2,256,1280]{2,1,0:T(8,128)}, u32[]{:S(2)}) copy-start(f32[2,256,1280]{2,1,0:T(8,128)} %copy-done) | copy-start | bytes 7864324
  2008.2 96.1 %copy-start.51 = (f32[1280]{0:T(1024)S(1)}, f32[1280]{0:T(1024)}, u32[]{:S(2)}) copy-start(f32[1280]{0:T(1024)} %copy-done.50) | copy-start | bytes 15364
  2008.2 96.1 %copy-start.53 = (f32[2,256]{1,0:T(2,128)S(1)}, f32[2,256]{1,0:T(2,128)}, u32[]{:S(2)}) copy-start(f32[2,256]{1,0:T(2,128)} %copy-done.52) | copy-start | bytes 6148
  2179.7 190.9 %reduce-scatter.21.cloned.1.call-start = ((), (), s32[]{:S(2)}) async-start(), calls=%async_computation.22 | async-start | bytes 6553600 | tf_op jit(solution)/shard_map/reduce_scatter | solution.py:229
  2203.5 27.9 copy-start.17
  2250.6 184.7 %reduce-scatter.39.cloned.1.call-start = ((), (), s32[]{:S(2)}) async-start(), calls=%async_computation.31 | async-start | bytes 4096000 | tf_op jit(solution)/shard_map/reduce_scatter | solution.py:287
  2255.9 244.8 %reduce-scatter.27.cloned.1.call-start = ((), (), s32[]{:S(2)}) async-start(), calls=%async_computation.25 | async-start | bytes 4096000 | tf_op jit(solution)/shard_map/reduce_scatter | solution.py:272
  2261.2 304.2 %reduce-scatter.35.cloned.1.call-start = ((), (), s32[]{:S(2)}) async-start(), calls=%async_computation.29 | async-start | bytes 4096000 | tf_op jit(solution)/shard_map/reduce_scatter | solution.py:281
  2266.2 363.9 %reduce-scatter.37.cloned.1.call-start = ((), (), s32[]{:S(2)}) async-start(), calls=%async_computation.30 | async-start | bytes 4096000 | tf_op jit(solution)/shard_map/reduce_scatter | solution.py:287
  2272.5 422.9 %reduce-scatter.31.cloned.1.call-start = ((), (), s32[]{:S(2)}) async-start(), calls=%async_computation.27 | async-start | bytes 4096000 | tf_op jit(solution)/shard_map/reduce_scatter | solution.py:278
  2277.4 483.1 %reduce-scatter.25.cloned.1.call-start = ((), (), s32[]{:S(2)}) async-start(), calls=%async_computation.24 | async-start | bytes 4096000 | tf_op jit(solution)/shard_map/reduce_scatter | solution.py:272
  2293.9 690.2 %reduce-scatter.43.cloned.1.call-start = ((), (), s32[]{:S(2)}) async-start(), calls=%async_computation.33 | async-start | bytes 16384000 | tf_op jit(solution)/shard_map/reduce_scatter | solution.py:299
  2307.6 900.3 %reduce-scatter.47.cloned.1.call-start = ((), (), s32[]{:S(2)}) async-start(), calls=%async_computation.35 | async-start | bytes 16384000 | tf_op jit(solution)/shard_map/reduce_scatter | solution.py:305
  2322.9 950.3 %reduce-scatter.33.cloned.1.call-start = ((), (), s32[]{:S(2)}) async-start(), calls=%async_computation.28 | async-start | bytes 4096000 | tf_op jit(solution)/shard_map/reduce_scatter | solution.py:281
  2328.0 1010.3 %reduce-scatter.29.cloned.1.call-start = ((), (), s32[]{:S(2)}) async-start(), calls=%async_computation.26 | async-start | bytes 4096000 | tf_op jit(solution)/shard_map/reduce_scatter | solution.py:278
  2375.7 1186.4 %reduce-scatter.41.cloned.1.call-start = ((), (), s32[]{:S(2)}) async-start(), calls=%async_computation.32 | async-start | bytes 16384000 | tf_op jit(solution)/shard_map/reduce_scatter | solution.py:299
  2389.4 1396.6 %reduce-scatter.45.cloned.1.call-start = ((), (), s32[]{:S(2)}) async-start(), calls=%async_computation.34 | async-start | bytes 16384000 | tf_op jit(solution)/shard_map/reduce_scatter | solution.py:305
  2402.0 1646.1 %all-reduce.40.cloned.1.call-start = ((), (), s32[]{:S(2)}) async-start(), calls=%async_computation.48 | async-start | bytes 39321600 | tf_op jit(solution)/shard_map/psum | solution.py:319
  3798.9 48.7 %copy-start.77 = (f32[2,256]{1,0:T(2,128)S(1)}, f32[2,256]{1,0:T(2,128)}, u32[]{:S(2)}) copy-start(f32[2,256]{1,0:T(2,128)} %copy-done.76) | copy-start | bytes 6148
  (99 other events, 476.6 us)
Sparse Core Ops, SparseCore 0:
  10.2 66.4 all-gather.58
  78.8 64.3 all-gather.54
  145.3 64.5 all-gather.56
  211.9 96.4 all-gather.48
  310.4 96.4 all-gather.46
  408.9 64.2 all-gather.60
  475.3 225.0 all-gather.62
  702.6 224.9 all-gather.64
  929.1 64.1 all-gather.66
  994.8 64.2 all-gather.70
  1060.7 64.5 all-gather.68
  1127.3 96.4 all-gather.50
  1225.3 96.4 all-gather.52
  1323.2 64.2 all-gather.72
  1389.5 225.0 all-gather.74
  1616.5 224.9 all-gather.76
  1908.7 94.7 reduce-scatter.18
  2005.7 94.2 reduce-scatter.16
  2179.9 94.2 reduce-scatter.22
  2276.3 94.2 reduce-scatter.20
  2372.9 62.3 reduce-scatter.38
  2438.2 62.3 reduce-scatter.26
  2503.0 62.3 reduce-scatter.34
  2567.6 62.3 reduce-scatter.36
  2632.9 62.3 reduce-scatter.30
  2698.1 62.3 reduce-scatter.24
  2763.3 220.8 reduce-scatter.42
  2986.5 221.3 reduce-scatter.46
  3210.2 62.9 reduce-scatter.32
  3275.9 62.3 reduce-scatter.28
  3341.3 220.8 reduce-scatter.40
  3564.5 221.3 reduce-scatter.44
  3792.0 256.0 all-reduce.39
where the time goes:
time: 4090 us; the launch traced here: 4080 us
  waiting for transfers between devices  3200 us (78%)
  matrix products  486 us (12%)
  other arithmetic  158 us (4%)
  local copies, waits for them, and re-layouts  131 us (3%)
  blocking collectives  79.1 us (2%)
    reduce_scatter x2, waiting for transfers between devices, backward_layer(): lax.psum_scatter(grad_down.astype(jnp.bfloat16), 'shard', scatter_dimensi...  447 us
    reduce_scatter x2, waiting for transfers between devices, backward_layer(): lax.psum_scatter(grad_up.astype(jnp.bfloat16), 'shard', scatter_dimension...  447 us
    all_gather x2, waiting for transfers between devices, fetch_forward(): lax.all_gather(local_params[11], 'shard', axis=0, tiled=True)  442 us
    all_gather x2, waiting for transfers between devices, fetch_forward(): lax.all_gather(local_params[13], 'shard', axis=0, tiled=True)  354 us
    all_gather x2, waiting for transfers between devices, forward_layer(): lax.all_gather(key_low, 'shard', axis=1, tiled=True)  182 us
    psum x1, waiting for transfers between devices, replica_layer(): lax.psum(owned_grads[2].astype(jnp.bfloat16), 'rep').astype(jnp.float32)  180 us
    all_gather x2, waiting for transfers between devices, forward_layer(): lax.all_gather(value_low, 'shard', axis=1, tiled=True)  163 us
    reduce_scatter x2, waiting for transfers between devices, backward_layer(): lax.psum_scatter(key_part.reshape(clip_count, length_all, model_width).as...  134 us
  transfers between devices with their start and end apart: 33, of which 32 were waited for; matrix products, arithmetic and copies ran while one was open for 14% of the time, Pallas kernels for 0%

commit v1 on v0

--- a/solution.py
+++ b/solution.py
@@ -1,13 +1,19 @@
+import functools
+import math
+
 import jax
 import jax.numpy as jnp
 from jax import lax
+from jax.experimental import pallas as pl
+from jax.experimental.pallas import tpu as pltpu
 from jax.sharding import PartitionSpec as P
 
 H = 16
-
-
 EPSILON = 1e-05
 NEGATIVE = -1e30
+BF16 = jnp.bfloat16
+F32 = jnp.float32
+BOTH = ("rep", "shard")
 
 
 def norm_affine(values, norm_gain, norm_shift):
@@ -332,7 +338,7 @@
     )
 
 
-def shards(
+def general_shards(
     inputs,
     lengths,
     cotangent,
@@ -419,7 +425,523 @@
     )
 
 
+def device_index(a, b, core, z):
+    return ((a * 2 + b) * 2 + core) * 4 + z
+
+
+def make_pairs(target):
+    return [
+        (device_index(a, b, core, z), device_index(*target(a, b, core, z)))
+        for a in range(2)
+        for b in range(2)
+        for core in range(2)
+        for z in range(4)
+    ]
+
+
+PAIRS = {
+    "a": make_pairs(lambda a, b, c, z: (1 - a, b, c, z)),
+    "b": make_pairs(lambda a, b, c, z: (a, 1 - b, c, z)),
+    "ab": make_pairs(lambda a, b, c, z: (1 - a, 1 - b, c, z)),
+    "core": make_pairs(lambda a, b, c, z: (a, b, 1 - c, z)),
+    "z1": make_pairs(lambda a, b, c, z: (a, b, c, (z + 1) % 4)),
+    "z2": make_pairs(lambda a, b, c, z: (a, b, c, (z + 2) % 4)),
+    "z3": make_pairs(lambda a, b, c, z: (a, b, c, (z + 3) % 4)),
+}
+for step in range(2):
+    PAIRS["in%d" % step] = make_pairs(
+        lambda a, b, c, z, step=step: (a, b, z // 2, 2 * c + (z + step) % 2)
+    )
+    PAIRS["out%d" % step] = [(target, source) for source, target in PAIRS["in%d" % step]]
+
+
+def send(values, way):
+    return lax.ppermute(values, BOTH, PAIRS[way])
+
+
+def pick(values, index, axis=0):
+    return lax.dynamic_index_in_dim(values, index, axis, keepdims=False)
+
+
+def place():
+    rep = lax.axis_index("rep")
+    return rep // 4, (rep // 2) % 2, rep % 2, lax.axis_index("shard")
+
+
+def after(values, *others):
+    return lax.optimization_barrier((values,) + others)[0]
+
+
+def own_piece(kind, shards):
+    a, b, core, z = place()
+    chip = a * 2 + b
+    if kind == "attn":
+        stacked = jnp.stack(shards)
+        return lax.dynamic_slice(stacked, (0, chip * 80, core * 640), (4, 80, 640))
+    if kind == "up":
+        part = lax.dynamic_slice(shards[0], (chip * 80, core * 2560), (80, 2560))
+        return jnp.stack([part[:, :1280], part[:, 1280:]])
+    part = lax.dynamic_slice(shards[0], (chip * 320, core * 640), (320, 640))
+    return part.reshape(2, 160, 640)
+
+
+def assemble_kernel(kind, count, *refs):
+    shards, refs = refs[:count], refs[count:]
+    sources, refs = refs[:10], refs[10:]
+    outs, sem = refs[:-1], refs[-1]
+    rep = lax.axis_index("rep")
+    a, b, core, z = rep // 4, (rep // 2) % 2, rep % 2, lax.axis_index("shard")
+    copies = []
+    rows = shards[0].shape[0]
+    for shard, out in zip(shards, outs):
+        at = pl.ds(pl.multiple_of(z * rows, rows), rows)
+        copies.append(pltpu.make_async_copy(shard, out.at[at, :], sem))
+    for number, source in enumerate(sources):
+        place_core = core if number < 5 else 1 - core
+        which = number % 5
+        chip_a = a if which in (0, 1) else 1 - a
+        chip_b = b if which in (0, 2) else 1 - b
+        chip = chip_a * 2 + chip_b
+        first = 0
+        if which == 4:
+            first = 2 if kind == "attn" else 1
+        for s in range(3):
+            from_z = lax.rem(z + 3 - s, 4)
+            for part in range(source.shape[1]):
+                unit = first + part
+                if kind == "attn":
+                    out = outs[unit]
+                    row, height = from_z * 320 + chip * 80, 80
+                    column, width = place_core * 640, 640
+                elif kind == "up":
+                    out = outs[0]
+                    row, height = from_z * 320 + chip * 80, 80
+                    column, width = place_core * 2560 + unit * 1280, 1280
+                else:
+                    out = outs[0]
+                    row, height = from_z * 1280 + chip * 320 + unit * 160, 160
+                    column, width = place_core * 640, 640
+                at = (
+                    pl.ds(pl.multiple_of(row, 16), height),
+                    pl.ds(pl.multiple_of(column, 128), width),
+                )
+                copies.append(pltpu.make_async_copy(source.at[s, part], out.at[at], sem))
+    for copy in copies:
+        copy.start()
+    for copy in copies:
+        copy.wait()
+
+
+def assemble(kind, shards, sources):
+    shape = {"attn": (1280, 1280), "up": (1280, 5120), "down": (5120, 1280)}[kind]
+    count = len(shards)
+    size = 2 * count * shape[0] * shape[1]
+    return pl.pallas_call(
+        functools.partial(assemble_kernel, kind, count),
+        out_shape=tuple(jax.ShapeDtypeStruct(shape, BF16) for _ in shards),
+        in_specs=[pl.BlockSpec(memory_space=pl.ANY)] * (count + 10),
+        out_specs=tuple(pl.BlockSpec(memory_space=pl.ANY) for _ in shards),
+        scratch_shapes=[pltpu.SemaphoreType.DMA],
+        cost_estimate=pl.CostEstimate(flops=0, bytes_accessed=2 * size, transcendentals=0),
+        name="assemble_" + kind,
+    )(*shards, *sources)
+
+
+def fetch(kind, shards, gate):
+    piece = own_piece(kind, shards)
+    if gate is not None:
+        piece = after(piece, gate)
+    far = jnp.stack([send(piece, "z1"), send(piece, "z2"), send(piece, "z3")])
+    half = far.shape[1] // 2
+    from_b, from_a = send(far, "b"), send(far, "a")
+    first, second = send(from_b[:, :half], "a"), send(from_a[:, half:], "b")
+    mine = (far, from_b, from_a, first, second)
+    other = tuple(send(part, "core") for part in mine)
+    return assemble(kind, shards, mine + other), far
+
+
+def attend_kernel(q, k0, k1, v0, v1, m0, m1, out, lse):
+    contract = (((0,), (0,)), ((), ()))
+    query = q[...]
+    s0 = lax.dot_general(k0[...], query, contract, preferred_element_type=F32) + m0[...]
+    s1 = lax.dot_general(k1[...], query, contract, preferred_element_type=F32) + m1[...]
+    top = jnp.maximum(jnp.max(s0, axis=0, keepdims=True), jnp.max(s1, axis=0, keepdims=True))
+    e0, e1 = jnp.exp(s0 - top), jnp.exp(s1 - top)
+    total = jnp.sum(e0, axis=0, keepdims=True) + jnp.sum(e1, axis=0, keepdims=True)
+    context = jnp.dot(v0[...], e0.astype(BF16), preferred_element_type=F32)
+    context += jnp.dot(v1[...], e1.astype(BF16), preferred_element_type=F32)
+    out[...] = (context / total).astype(BF16)
+    lse[0] = top + jnp.log(total)
+
+
+def head_spec(rows, columns):
+    return pl.BlockSpec((rows, columns), lambda h: (h, 0))
+
+
+def whole_spec(rows, columns):
+    return pl.BlockSpec((rows, columns), lambda h: (0, 0))
+
+
+def attend(query, key, value, far_key, far_value, mask, far_mask):
+    width, count = query.shape
+    size = width // H
+    heads = head_spec(size, count)
+    masks = whole_spec(count, 1)
+    return pl.pallas_call(
+        attend_kernel,
+        grid=(H,),
+        out_shape=(
+            jax.ShapeDtypeStruct((width, count), BF16),
+            jax.ShapeDtypeStruct((H, 1, count), F32),
+        ),
+        in_specs=[heads] * 5 + [masks] * 2,
+        out_specs=(heads, pl.BlockSpec((1, 1, count), lambda h: (h, 0, 0))),
+        compiler_params=pltpu.CompilerParams(vmem_limit_bytes=48 << 20),
+        cost_estimate=pl.CostEstimate(
+            flops=8 * width * count * count * 3,
+            bytes_accessed=12 * width * count,
+            transcendentals=2 * H * count * count,
+        ),
+        name="attend",
+    )(query, key, far_key, value, far_value, mask, far_mask)
+
+
+def attend_back_kernel(q, k0, k1, v0, v1, m0, m1, lse, g, gq, gk0, gk1, gv0, gv1):
+    outer = (((0,), (0,)), ((), ()))
+    inner = (((1,), (1,)), ((), ()))
+    query, grad, norm = q[...], g[...], lse[0]
+    halves = []
+    delta = None
+    for k, v, m, gv in ((k0, v0, m0, gv0), (k1, v1, m1, gv1)):
+        s = lax.dot_general(k[...], query, outer, preferred_element_type=F32) + m[...]
+        p = jnp.exp(s - norm)
+        dp = lax.dot_general(v[...], grad, outer, preferred_element_type=F32)
+        part = jnp.sum(p * dp, axis=0, keepdims=True)
+        delta = part if delta is None else delta + part
+        gv[...] = lax.dot_general(
+            grad, p.astype(BF16), inner, preferred_element_type=F32
+        ).astype(BF16)
+        halves.append((p, dp))
+    total = None
+    for (p, dp), k, gk in zip(halves, (k0, k1), (gk0, gk1)):
+        ds = (p * (dp - delta)).astype(BF16)
+        part = jnp.dot(k[...], ds, preferred_element_type=F32)
+        total = part if total is None else total + part
+        gk[...] = lax.dot_general(query, ds, inner, preferred_element_type=F32).astype(BF16)
+    gq[...] = total.astype(BF16)
+
+
+def attend_back(query, key, value, far_key, far_value, mask, far_mask, lse, grad):
+    width, count = query.shape
+    size = width // H
+    heads = head_spec(size, count)
+    masks = whole_spec(count, 1)
+    stats = pl.BlockSpec((1, 1, count), lambda h: (h, 0, 0))
+    return pl.pallas_call(
+        attend_back_kernel,
+        grid=(H,),
+        out_shape=tuple(jax.ShapeDtypeStruct((width, count), BF16) for _ in range(5)),
+        in_specs=[heads] * 5 + [masks] * 2 + [stats, heads],
+        out_specs=tuple(heads for _ in range(5)),
+        compiler_params=pltpu.CompilerParams(vmem_limit_bytes=48 << 20),
+        cost_estimate=pl.CostEstimate(
+            flops=20 * width * count * count * 3,
+            bytes_accessed=22 * width * count,
+            transcendentals=2 * H * count * count,
+        ),
+        name="attend_back",
+    )(query, key, far_key, value, far_value, mask, far_mask, lse, grad)
+
+
+def add(*parts):
+    total = parts[0].astype(F32)
+    for part in parts[1:]:
+        total = total + part.astype(F32)
+    return total.astype(BF16)
+
+
+def reduce_blocks(blocks, cut):
+    a, b, core, z = place()
+    first, second = blocks[..., :cut], blocks[..., cut:]
+    got = send(pick(first, 1 - b, 2), "b")
+    first = add(pick(first, b, 2), got)
+    got = send(pick(second, 1 - a, 1), "a")
+    second = add(pick(second, a, 1), got)
+    got = send(pick(first, 1 - a, 1), "a")
+    first = add(pick(first, a, 1), got)
+    got = send(pick(second, 1 - b, 1), "b")
+    second = add(pick(second, b, 1), got)
+    both = jnp.concatenate([first, second], axis=-1)
+    got = [send(pick(both, (z + s) % 4), "z%d" % s) for s in (1, 2, 3)]
+    return add(pick(both, z), *got)
+
+
+def spread(piece):
+    a, b, core, z = place()
+    parts = jnp.stack([piece, send(piece, "b"), send(piece, "a"), send(piece, "ab")])
+    other = send(parts, "core")
+    me = core * 4 + a * 2 + b
+    every = jnp.concatenate([parts, other])
+    ordered = jnp.stack([pick(every, jnp.bitwise_xor(me, i)) for i in range(8)])
+    return ordered.reshape(2, 4, *piece.shape)
+
+
+def product(left, right, spec):
+    return jnp.einsum(spec, left, right, preferred_element_type=F32)
+
+
+def half_columns(values, core):
+    size = values.shape[1] // 2
+    return lax.dynamic_slice_in_dim(values, core * size, size, 1)
+
+
+def half_rows(values, core):
+    size = values.shape[0] // 2
+    return lax.dynamic_slice_in_dim(values, core * size, size, 0)
+
+
+def normalize(values):
+    center = values - jnp.mean(values, axis=-1, keepdims=True)
+    scale = lax.rsqrt(jnp.mean(center * center, axis=-1, keepdims=True) + EPSILON)
+    return center * scale, scale
+
+
+def norm_back(grad, gain, unit, scale):
+    e = grad * gain
+    return scale * (
+        e
+        - jnp.mean(e, axis=-1, keepdims=True)
+        - unit * jnp.mean(e * unit, axis=-1, keepdims=True)
+    )
+
+
+ROOT_HALF = math.sqrt(0.5)
+ROOT_TWO_PI = math.sqrt(2.0 * math.pi)
+
+
+def forward_fast(state, weights, vectors, masks):
+    query_weight, key_weight, value_weight, out_weight, up_weight, down_weight = weights
+    (attn_gain, attn_shift, query_bias, value_bias, out_bias, mlp_gain, mlp_shift, down_bias,
+     up_bias) = vectors
+    scale = float(state.shape[1] // H) ** (-0.5)
+    unit, _ = normalize(state)
+    normed = (unit * attn_gain + attn_shift).astype(BF16)
+    key = product(key_weight, normed, "df,sd->fs").astype(BF16)
+    value = (product(value_weight, normed, "df,sd->fs") + value_bias[:, None]).astype(BF16)
+    far_key, far_value = send(key, "core"), send(value, "core")
+    query = ((product(query_weight, normed, "df,sd->fs") + query_bias[:, None]) * scale).astype(BF16)
+    context, lse = attend(query, key, value, far_key, far_value, *masks)
+    middle = state + product(context, out_weight, "fs,fd->sd") + out_bias
+    unit, _ = normalize(middle)
+    hidden_in = (unit * mlp_gain + mlp_shift).astype(BF16)
+    pre_gelu = product(hidden_in, up_weight, "sd,df->sf") + up_bias
+    active = (pre_gelu * (0.5 * (1.0 + lax.erf(pre_gelu * ROOT_HALF)))).astype(BF16)
+    result = middle + product(active, down_weight, "sf,fd->sd") + down_bias
+    kept = (normed, query, key, value, far_key, far_value, lse, context, middle, hidden_in, pre_gelu,
+            active)
+    return result, kept
+
+
+def two(own, core, cut):
+    return jnp.concatenate([cut(own, core), send(cut(own, 1 - core), "core")], axis=0)
+
+
+def backward_fast(state, grad_after, weights, vectors, masks, kept):
+    query_weight, key_weight, value_weight, out_weight, up_weight, down_weight = weights
+    (attn_gain, attn_shift, query_bias, value_bias, out_bias, mlp_gain, mlp_shift, down_bias,
+     up_bias) = vectors
+    (normed, query, key, value, far_key, far_value, lse, context, middle, hidden_in, pre_gelu,
+     active) = kept
+    a, b, core, z = place()
+    scale = float(state.shape[1] // H) ** (-0.5)
+    count = state.shape[0]
+
+    def whole(values):
+        return jnp.concatenate([values, send(values, "core")], axis=0)
+
+    def active_part(values, which):
+        return pick(values.reshape(count, 4, 2, 640), which, 2).reshape(count, 2560)
+
+    grad_f = grad_after.astype(BF16)
+    active_both = two(active, core, active_part)
+    grad_f_both = whole(grad_f)
+    grad_down = product(active_both, grad_f_both, "sa,sb->ab").astype(BF16)
+    grad_down = spread(reduce_blocks(grad_down.reshape(4, 2, 2, 160, 1280), 640))
+    grad_down = grad_down.reshape(1280, 1280)
+
+    grad_active = product(grad_f, down_weight, "sd,fd->sf")
+    slope = 0.5 * (1.0 + lax.erf(pre_gelu * ROOT_HALF)) + pre_gelu * jnp.exp(
+        -0.5 * pre_gelu * pre_gelu
+    ) * (1.0 / ROOT_TWO_PI)
+    grad_pre = (grad_active * slope).astype(BF16)
+    grad_pre_both = two(grad_pre, core, half_columns)
+    hidden_both = whole(hidden_in)
+    grad_up = product(hidden_both, grad_pre_both, "sa,sb->ab").astype(BF16)
+    grad_up = spread(reduce_blocks(grad_up.reshape(4, 2, 2, 80, 2560), 1280))
+    grad_up = grad_up.transpose(1, 2, 0, 3).reshape(320, 5120)
+
+    grad_hidden = product(grad_pre, up_weight, "sf,df->sd")
+    unit, spread_scale = normalize(middle)
+    grad_middle = grad_after + norm_back(grad_hidden, mlp_gain, unit, spread_scale)
+    grad_o = grad_middle.astype(BF16)
+    mlp_gain_grad, mlp_shift_grad = jnp.sum(grad_hidden * unit, 0), jnp.sum(grad_hidden, 0)
+
+    context_both = jnp.concatenate([context, send(context, "core")], axis=1)
+    grad_o_both = two(grad_o, core, half_columns)
+    grad_out = product(context_both, grad_o_both, "as,sb->ab").astype(BF16)
+    grad_out = spread(reduce_blocks(grad_out.reshape(4, 2, 2, 80, 640), 384))
+    grad_out = grad_out.transpose(1, 2, 0, 3).reshape(320, 1280)
+
+    grad_context = product(out_weight, grad_o, "fd,sd->fs").astype(BF16)
+    grad_query, grad_key, far_grad_key, grad_value, far_grad_value = attend_back(
+        query, key, value, far_key, far_value, *masks, lse, grad_context
+    )
+    grad_key = add(grad_key, send(far_grad_key, "core"))
+    grad_value = add(grad_value, send(far_grad_value, "core"))
+    normed_both = whole(normed)
+    parts = jnp.concatenate(
+        [
+            jnp.concatenate([half_rows(g, core), send(half_rows(g, 1 - core), "core")], axis=1)
+            for g in (grad_query, grad_key, grad_value)
+        ],
+        axis=0,
+    )
+    grad_qkv = product(normed_both, parts, "sa,bs->ab")
+    columns = jnp.arange(1920) < 640
+    grad_qkv = (grad_qkv * jnp.where(columns, scale, 1.0)).astype(BF16)
+    grad_qkv = spread(reduce_blocks(grad_qkv.reshape(4, 2, 2, 80, 1920), 1024))
+    grad_qkv = grad_qkv.reshape(2, 4, 80, 3, 640).transpose(3, 1, 2, 0, 4).reshape(3, 320, 1280)
+
+    grad_normed = (
+        product(grad_query, query_weight, "fs,df->sd") * scale
+        + product(grad_key, key_weight, "fs,df->sd")
+        + product(grad_value, value_weight, "fs,df->sd")
+    )
+    unit, spread_scale = normalize(state)
+    attn_gain_grad, attn_shift_grad = jnp.sum(grad_normed * unit, 0), jnp.sum(grad_normed, 0)
+    grad_before = grad_middle + norm_back(grad_normed, attn_gain, unit, spread_scale)
+
+    def rows(values):
+        return jnp.sum(values.astype(F32), axis=0)
+
+    small = jnp.concatenate(
+        [
+            attn_gain_grad,
+            attn_shift_grad,
+            jnp.sum(grad_query.astype(F32), axis=1) * scale,
+            jnp.sum(grad_value.astype(F32), axis=1),
+            rows(grad_o),
+            mlp_gain_grad,
+            mlp_shift_grad,
+            rows(grad_f),
+            rows(grad_pre),
+        ]
+    )
+    return grad_before, (grad_qkv, grad_out, grad_up, grad_down), small
+
+
+def plane_shards(
+    inputs, lengths, cotangent, attn_gain, attn_shift, query_weight, query_bias, key_weight,
+    value_weight, value_bias, out_weight, out_bias, mlp_gain, mlp_shift, up_weight, up_bias,
+    down_weight, down_bias,
+):
+    a, b, core, z = place()
+    layers = attn_gain.shape[0]
+    block = inputs.shape[1]
+
+    def gather_tokens(values):
+        return jnp.concatenate(
+            [send(pick(values, (z + step) % 2), "in%d" % step) for step in range(2)], axis=0
+        )
+
+    def return_tokens(values):
+        got = [send(values[step * block : (step + 1) * block], "out%d" % step) for step in range(2)]
+        got = jnp.stack(got)
+        return jnp.stack([pick(got, (z + clip) % 2) for clip in range(2)])
+
+    packed = jnp.concatenate(
+        [attn_gain, attn_shift, query_bias, value_bias, out_bias, mlp_gain, mlp_shift, down_bias,
+         up_bias], axis=1,
+    )
+    pieces = jnp.stack([packed] + [send(packed, "z%d" % s) for s in (1, 2, 3)])
+    pieces = jnp.stack([pick(pieces, (z + 4 - from_z) % 4) for from_z in range(4)]).astype(F32)
+    vectors = []
+    for layer in range(layers):
+        row = [pieces[:, layer, i * 320 : (i + 1) * 320].reshape(1280) for i in range(8)]
+        row.append(pieces[:, layer, 2560:].reshape(5120))
+        vectors.append(tuple(row))
+
+    state = gather_tokens(inputs).astype(F32)
+
+    far_lengths = send(lengths, "core")
+    four = jnp.where(core == 0, jnp.concatenate([lengths, far_lengths]),
+                     jnp.concatenate([far_lengths, lengths]))
+    length = pick(four, z)
+
+    def positions(which):
+        return jnp.concatenate(
+            [(2 * which + (z + step) % 2) * block + jnp.arange(block) for step in range(2)]
+        )
+
+    def mask_of(which):
+        return jnp.where(positions(which) < length, 0.0, NEGATIVE).astype(F32)[:, None]
+
+    masks = (mask_of(core), mask_of(1 - core))
+
+    weights = []
+    gate = None
+    for layer in range(layers):
+        attn, gate = fetch(
+            "attn", (query_weight[layer], key_weight[layer], value_weight[layer], out_weight[layer]), gate
+        )
+        up, gate = fetch("up", (up_weight[layer],), gate)
+        down, gate = fetch("down", (down_weight[layer],), gate)
+        weights.append(attn + up + down)
+
+    states, kept = [], []
+    for layer in range(layers):
+        states.append(state)
+        state, values = forward_fast(state, weights[layer], vectors[layer], masks)
+        kept.append(values)
+    output = return_tokens(state.astype(BF16))
+
+    row_mask = (positions(core) < length).astype(F32)
+    grad = gather_tokens(cotangent).astype(F32) * row_mask[:, None]
+    small, large = [None] * layers, [None] * layers
+    for layer in reversed(range(layers)):
+        grad, large[layer], small[layer] = backward_fast(
+            states[layer], grad, weights[layer], vectors[layer], masks, kept[layer]
+        )
+    input_grad = return_tokens(grad.astype(BF16)).astype(F32)
+
+    total = lax.psum(jnp.stack(small), BOTH)
+    vec = pick(total[:, :10240].reshape(layers, 8, 4, 320), z, 2)
+    up_bias_grad = pick(total[:, 10240:].reshape(layers, 4, 1280), z, 1)
+
+    def stack(parts):
+        return jnp.stack([part.astype(F32) for part in parts])
+
+    query_grad = stack([g[0][0] for g in large])
+    key_grad = stack([g[0][1] for g in large])
+    value_grad = stack([g[0][2] for g in large])
+    out_grad = stack([g[1] for g in large])
+    up_grad = stack([g[2] for g in large])
+    down_grad = stack([g[3] for g in large])
+    return (
+        output, input_grad, vec[:, 0], vec[:, 1], query_grad, vec[:, 2], key_grad, value_grad,
+        vec[:, 3], out_grad, vec[:, 4], vec[:, 5], vec[:, 6], up_grad, up_bias_grad, down_grad,
+        vec[:, 7],
+    )
+
+
+def pick_body(mesh):
+    if mesh.shape["rep"] == 8 and mesh.shape["shard"] == 4:
+        return plane_shards
+    return general_shards
+
+
 def solution(mesh):
+    body = pick_body(mesh)
     placed = (
         P("rep", "shard", None),
         P("rep"),
@@ -441,7 +963,7 @@
         P(None, "shard"),
     )
     return jax.shard_map(
-        shards,
+        body,
         mesh=mesh,
         in_specs=placed,
         out_specs=(

time: 4090 us -> 4280 us (1.046)
  Pallas kernels: 0 us -> 2490 us
  waiting for transfers between devices: 3200 us -> 813 us
  starting transfers between devices: 2.39 us -> 261 us
  matrix products: 486 us -> 230 us
  local copies, waits for them, and re-layouts: 131 us -> 361 us
  blocking collectives: 79.1 us -> 0 us
  other arithmetic: 158 us -> 102 us
    pallas_call x0 -> x10, Pallas kernels: none -> 2490 us  [the longest x6 2390 us: assemble(): pl.pallas_call(functools.partial(assemble_kernel, kind, count), out_shape...]
    reduce_scatter x16 -> x0, waiting for transfers between devices: 1530 us -> none  [the longest x2 447 us: backward_layer(): lax.psum_scatter(grad_down.astype(jnp.bfloat16), 'shard', scatter_dimensi...]
    all_gather x16 -> x0, waiting for transfers between devices: 1490 us -> none  [the longest x2 442 us: fetch_forward(): lax.all_gather(local_params[11], 'shard', axis=0, tiled=True)]
    ppermute x0 -> x200, waiting for transfers between devices: none -> 737 us  [send(): return lax.ppermute(values, BOTH, PAIRS[way])]
    ppermute x0 -> x200, starting transfers between devices: none -> 261 us  [send(): return lax.ppermute(values, BOTH, PAIRS[way])]
    dot_general x46 -> x32, matrix products: 450 us -> 230 us  [product(): return jnp.einsum(spec, left, right, preferred_element_type=F32)]
    psum x1, waiting for transfers between devices: 180 us -> 76.3 us  [plane_shards(): total = lax.psum(jnp.stack(small), BOTH)]
    convert_element_type x26 -> x42, other arithmetic: 111 us -> 26.5 us  [the longest x34 17.2 us: add(): return total.astype(BF16)]
  transfers between devices with their start and end apart: 33 -> 201, of which waited for: 32 -> 65; matrix products, arithmetic and copies ran while one was open for 14% -> 15% of each run, Pallas kernels for 0% -> 58%
where the time goes in v1:
time: 4280 us; the launch traced here: 4270 us
  Pallas kernels  2490 us (58%)
  waiting for transfers between devices  813 us (19%)
  local copies, waits for them, and re-layouts  361 us (8%)
  starting transfers between devices  261 us (6%)
  matrix products  230 us (5%)
  other arithmetic  102 us (2%)
    pallas_call x6, Pallas kernels, assemble(): pl.pallas_call(functools.partial(assemble_kernel, kind, count), out_shape...  2390 us
    ppermute x200, waiting for transfers between devices, send(): return lax.ppermute(values, BOTH, PAIRS[way])  737 us
    ppermute x200, starting transfers between devices, send(): return lax.ppermute(values, BOTH, PAIRS[way])  261 us
    dot_general x32, matrix products, product(): return jnp.einsum(spec, left, right, preferred_element_type=F32)  230 us
    unnamed x517, local copies, waits for them, and re-layouts  124 us
  transfers between devices with their start and end apart: 201, of which 65 were waited for; matrix products, arithmetic and copies ran while one was open for 15% of the time, Pallas kernels for 58%

profile of v1, /device:TPU:11, one launch (start us, length us, event | category | flops | bytes accessed | tf_op | source)
XLA Modules:
  0.0 4273.5 jit_solution(7776045221678486262)
XLA Ops:
  30.8 20.6 collective-permute-done.3
  66.7 24.6 collective-permute-done.21
  113.5 58.2 %collective-permute-done.33 = bf16[2,160,640]{2,1,0:T(8,128)(2,1)S(1)} collective-permute-done((bf16[2,160,640]{2,1,0:T(8,128)(2,1)S(1)}, bf16[2,160,640]{2,1,0:T(8,128)(2,1)S(1)}, u32[]{:S(2)}, u32[]{:S(2)}) %collective-permute-start.33) | collective-permute-done | bytes 409632 | tf_op jit(solution)/shard_map/ppermute | solution.py:459
  185.0 20.7 collective-permute-done.85
  211.7 12.1 collective-permute-done.46
  226.3 13.5 collective-permute-start.27
  244.9 24.7 collective-permute-done.59
  288.5 22.9 collective-permute-done.8.refs_8_
  317.2 20.0 collective-permute-done.71
  340.6 11.4 collective-permute-done.25.refs_4_
  365.1 14.0 collective-permute-done.47.refs_5_
  386.8 31.8 collective-permute-done.37.refs_4_
  432.7 9.8 collective-permute-done.49.refs_7_
  446.1 398.2 %assemble_attn.2 = (bf16[1280,1280]{1,0:T(8,128)(2,1)}, bf16[1280,1280]{1,0:T(8,128)(2,1)}, bf16[1280,1280]{1,0:T(8,128)(2,1)}, bf16[1280,1280]{1,0:T(8,128)(2,1)}) custom-call(bf16[320,1280]{1,0:T(8,128)(2,1)} %get-tuple-element.193.refs_0_, bf16[320,1280]{1,0:T(8,128)(2,1)} %get-tuple-element.286.refs_1_, bf16[320,1280]{1,0:T(8,128)(2,1)} %get-tuple-element.201.refs_2_, ...), custom_call_target="tpu_custom_call" | custom-call | bytes 26214400 | tf_op jit(solution)/shard_map/assemble_attn/pallas_call | solution.py:539
  875.9 398.2 %assemble_up.2 = bf16[1280,5120]{1,0:T(8,128)(2,1)} custom-call(bf16[320,5120]{1,0:T(8,128)(2,1)} %get-tuple-element.147.refs_0_, bf16[3,2,80,1280]{3,2,1,0:T(8,128)(2,1)} %copy-done.55, bf16[3,2,80,1280]{3,2,1,0:T(8,128)(2,1)} %collective-permute-done.23.refs_2_, bf16[3,2,80,1280]{3,2,1,0:T(8,128)(2,1)} %collective-permute-done.24.refs_3_, ...), custom_call_target="tpu_custom_call" | custom-call | bytes 26214400 | tf_op jit(solution)/shard_map/assemble_up/pallas_call | solution.py:539
  1278.0 398.2 %assemble_down.2 = bf16[5120,1280]{1,0:T(8,128)(2,1)} custom-call(bf16[1280,1280]{1,0:T(8,128)(2,1)} %get-tuple-element.143.refs_0_, bf16[3,2,160,640]{3,2,1,0:T(8,128)(2,1)} %copy-done.56, bf16[3,2,160,640]{3,2,1,0:T(8,128)(2,1)} %collective-permute-done.35.refs_2_, bf16[3,2,160,640]{3,2,1,0:T(8,128)(2,1)} %collective-permute-done.36.refs_3_, ...), custom_call_target="tpu_custom_call" | custom-call | bytes 26214400 | tf_op jit(solution)/shard_map/assemble_down/pallas_call | solution.py:539
  1677.5 398.2 %assemble_attn.3 = (bf16[1280,1280]{1,0:T(8,128)(2,1)}, bf16[1280,1280]{1,0:T(8,128)(2,1)}, bf16[1280,1280]{1,0:T(8,128)(2,1)}, bf16[1280,1280]{1,0:T(8,128)(2,1)}) custom-call(bf16[320,1280]{1,0:T(8,128)(2,1)} %get-tuple-element.194.refs_0_, bf16[320,1280]{1,0:T(8,128)(2,1)} %get-tuple-element.285.refs_1_, bf16[320,1280]{1,0:T(8,128)(2,1)} %get-tuple-element.202.refs_2_, ...), custom_call_target="tpu_custom_call" | custom-call | bytes 26214400 | tf_op jit(solution)/shard_map/assemble_attn/pallas_call | solution.py:539
  2078.1 19.0 attend.2
  2101.4 14.5 multiply_convert_fusion.1
  2115.9 9.4 fusion.273
  2130.9 10.3 collective-permute-done.76.refs_5_
  2145.3 12.9 reshape.528
  2164.8 12.2 constant_dynamic-slice_fusion.7
  2176.9 11.1 copy.173
  2188.1 11.1 copy.172
  2204.6 398.2 %assemble_up.3 = bf16[1280,5120]{1,0:T(8,128)(2,1)} custom-call(bf16[320,5120]{1,0:T(8,128)(2,1)} %get-tuple-element.148.refs_0_, bf16[3,2,80,1280]{3,2,1,0:T(8,128)(2,1)} %copy-done.54, bf16[3,2,80,1280]{3,2,1,0:T(8,128)(2,1)} %copy-done.76, bf16[3,2,80,1280]{3,2,1,0:T(8,128)(2,1)} %collective-permute-done.62.refs_3_, ...), custom_call_target="tpu_custom_call" | custom-call | bytes 26214400 | tf_op jit(solution)/shard_map/assemble_up/pallas_call | solution.py:539
  2603.3 398.2 %assemble_down.3 = bf16[5120,1280]{1,0:T(8,128)(2,1)} custom-call(bf16[1280,1280]{1,0:T(8,128)(2,1)} %get-tuple-element.144.refs_0_, bf16[3,2,160,640]{3,2,1,0:T(8,128)(2,1)} %pad_maximum_fusion.12.refs_1_, bf16[3,2,160,640]{3,2,1,0:T(8,128)(2,1)} %collective-permute-done.73.refs_2_, bf16[3,2,160,640]{3,2,1,0:T(8,128)(2,1)} %collective-permute-done.74.refs_3_, ...), custom_call_target="tpu_custom_call" | custom-call | bytes 26214400 | tf_op jit(solution)/shard_map/assemble_down/pallas_call | solution.py:539
  3002.8 20.2 attend.3
  3028.6 13.8 multiply_convert_fusion
  3042.4 16.6 convert_reduce_fusion
  3059.0 14.4 multiply_reduce_fusion
  3081.0 30.5 attend_back.2
  3113.0 12.4 reshape.532
  3125.5 13.5 constant_dynamic-slice_fusion.3
  3139.3 12.9 fusion.74
  3159.9 11.1 copy.178
  3170.9 11.1 copy.177
  3207.6 16.8 convert_reduce_fusion.1
  3224.4 14.9 multiply_reduce_fusion.2
  3260.7 30.0 attend_back.3
  3380.0 9.3 convolution_convert_fusion.1
  3402.4 9.3 convolution_convert_fusion
  3417.1 9.6 convolution_convert_fusion.2
  3438.1 76.3 %all-reduce.2.cloned.1.call-done = f32[2,15360]{1,0:T(2,128)} async-done(((f32[2,15360]{1,0:T(2,128)}), f32[2,15360]{1,0:T(2,128)}) %all-reduce.2.cloned.1.call-update) | async-done | bytes 122896 | tf_op jit(solution)/shard_map/psum | solution.py:917
  3565.1 13.7 collective-permute-done.91
  3594.3 29.4 collective-permute-done.114
  3625.7 9.4 convolution_convert_fusion.3
  3647.4 15.5 collective-permute-done.116
  3682.5 16.5 collective-permute-done.189
  3701.0 16.1 collective-permute-done.165
  3717.6 16.5 collective-permute-done.163
  3742.3 61.6 %collective-permute-done.118 = bf16[80,1920]{1,0:T(8,128)(2,1)S(1)} collective-permute-done((bf16[80,1920]{1,0:T(8,128)(2,1)S(1)}, bf16[80,1920]{1,0:T(8,128)(2,1)S(1)}, u32[]{:S(2)}, u32[]{:S(2)}) %collective-permute-start.118) | collective-permute-done | bytes 307232 | tf_op jit(solution)/shard_map/ppermute | solution.py:459
  3814.2 27.7 collective-permute-done.99
  3844.3 14.7 collective-permute-done.166
  3859.3 17.3 collective-permute-done.192
  3880.7 12.7 collective-permute-done.97
  3895.3 11.2 collective-permute-done.181
  3910.0 19.4 collective-permute-done.182
  3932.6 11.0 collective-permute-done.168
  3946.7 17.9 collective-permute-done.169
  3967.7 11.0 collective-permute-done.194
  3981.8 14.7 collective-permute-done.195
  4069.2 16.7 collective-permute-done.170
  4120.7 24.8 collective-permute-start.199
  (1188 shorter events, 781.2 us)
Async XLA Ops:
  7.2 3507.2 %all-reduce.2.cloned.1.call-start = ((), (), s32[]{:S(2)}) async-start(), calls=%async_computation | async-start | bytes 245760 | tf_op jit(solution)/shard_map/psum | solution.py:917
  19.0 81.4 %collective-permute-start.14 = (bf16[2,3840]{1,0:T(2,128)(2,1)S(1)}, bf16[2,3840]{1,0:T(2,128)(2,1)S(1)}, u32[]{:S(2)}, u32[]{:S(2)}) collective-permute-start(bf16[2,3840]{1,0:T(2,128)(2,1)S(1)} %concatenate.178), channel_id=1, source_target_pairs={{0,1},{1,2},{2,3},{3,0},{4,5},{5,6},{6,7},{7,4},{8,9},{9,10},{10,1... | collective-permute-start | bytes 46088 | tf_op jit(solution)/shard_map/ppermute | solution.py:459
  19.0 82.3 %collective-permute-start.15 = (bf16[2,3840]{1,0:T(2,128)(2,1)S(1)}, bf16[2,3840]{1,0:T(2,128)(2,1)S(1)}, u32[]{:S(2)}, u32[]{:S(2)}) collective-permute-start(bf16[2,3840]{1,0:T(2,128)(2,1)S(1)} %concatenate.178), channel_id=1, source_target_pairs={{0,2},{1,3},{2,0},{3,1},{4,6},{5,7},{6,4},{7,5},{8,10},{9,11},{10,... | collective-permute-start | bytes 46088 | tf_op jit(solution)/shard_map/ppermute | solution.py:459
  94.0 89.4 %collective-permute-start = (bf16[256,1280]{1,0:T(8,128)(2,1)S(1)}, bf16[256,1280]{1,0:T(8,128)(2,1)S(1)}, u32[]{:S(2)}, u32[]{:S(2)}) collective-permute-start(bf16[256,1280]{1,0:T(8,128)(2,1)S(1)} %get-tuple-element.234), channel_id=1, source_target_pairs={{0,0},{1,1},{2,4},{3,5},{4,2},{5,3},{6,6},{7,7},{8,8},{9,9},{10,12... | collective-permute-start | bytes 1966088 | tf_op jit(solution)/shard_map/ppermute | solution.py:459
  100.0 83.3 %collective-permute-start.1 = (bf16[256,1280]{1,0:T(8,128)(2,1)S(1)}, bf16[256,1280]{1,0:T(8,128)(2,1)S(1)}, u32[]{:S(2)}, u32[]{:S(2)}) collective-permute-start(bf16[256,1280]{1,0:T(8,128)(2,1)S(1)} %get-tuple-element.235), channel_id=1, source_target_pairs={{0,1},{1,0},{2,5},{3,4},{4,3},{5,2},{6,7},{7,6},{8,9},{9,8},{10,13... | collective-permute-start | bytes 1966088 | tf_op jit(solution)/shard_map/ppermute | solution.py:459
  100.3 71.3 %collective-permute-start.33 = (bf16[2,160,640]{2,1,0:T(8,128)(2,1)S(1)}, bf16[2,160,640]{2,1,0:T(8,128)(2,1)S(1)}, u32[]{:S(2)}, u32[]{:S(2)}) collective-permute-start(bf16[2,160,640]{2,1,0:T(8,128)(2,1)S(1)} %bitcast.607), channel_id=1, source_target_pairs={{0,2},{1,3},{2,0},{3,1},{4,6},{5,7},{6,4},{7,5},{8,10},{9,11},{10,... | collective-permute-start | bytes 1228808 | tf_op jit(solution)/shard_map/ppermute | solution.py:459
  101.3 70.4 %collective-permute-start.34 = (bf16[2,160,640]{2,1,0:T(8,128)(2,1)S(1)}, bf16[2,160,640]{2,1,0:T(8,128)(2,1)S(1)}, u32[]{:S(2)}, u32[]{:S(2)}) collective-permute-start(bf16[2,160,640]{2,1,0:T(8,128)(2,1)S(1)} %bitcast.608), channel_id=1, source_target_pairs={{0,3},{1,0},{2,1},{3,2},{4,7},{5,4},{6,5},{7,6},{8,11},{9,8},{10,9... | collective-permute-start | bytes 1228808 | tf_op jit(solution)/shard_map/ppermute | solution.py:459
  104.4 79.3 %collective-permute-start.84 = (bf16[256,1280]{1,0:T(8,128)(2,1)S(1)}, bf16[256,1280]{1,0:T(8,128)(2,1)S(1)}, u32[]{:S(2)}, u32[]{:S(2)}) collective-permute-start(bf16[256,1280]{1,0:T(8,128)(2,1)S(1)} %get-tuple-element.228), channel_id=1, source_target_pairs={{0,0},{1,1},{2,4},{3,5},{4,2},{5,3},{6,6},{7,7},{8,8},{9,9},{10,12... | collective-permute-start | bytes 1966088 | tf_op jit(solution)/shard_map/ppermute | solution.py:459
  208.8 64.0 %collective-permute-start.23 = (bf16[3,2,80,1280]{3,2,1,0:T(8,128)(2,1)S(1)}, bf16[3,2,80,1280]{3,2,1,0:T(8,128)(2,1)}, u32[]{:S(2)}, u32[]{:S(2)}) collective-permute-start(bf16[3,2,80,1280]{3,2,1,0:T(8,128)(2,1)S(1)} %pad_maximum_fusion.8.refs_1_), channel_id=1, source_target_pairs={{0,8},{1,9},{2,10},{3,11},{4,12},{5,13},{6,14},{7,15},{8,0},{9,1},... | collective-permute-start | bytes 3686408 | tf_op jit(solution)/shard_map/ppermute | solution.py:459
  223.9 50.2 %collective-permute-start.24 = (bf16[3,2,80,1280]{3,2,1,0:T(8,128)(2,1)S(1)}, bf16[3,2,80,1280]{3,2,1,0:T(8,128)(2,1)}, u32[]{:S(2)}, u32[]{:S(2)}) collective-permute-start(bf16[3,2,80,1280]{3,2,1,0:T(8,128)(2,1)S(1)} %pad_maximum_fusion.8.refs_1_), channel_id=1, source_target_pairs={{0,16},{1,17},{2,18},{3,19},{4,20},{5,21},{6,22},{7,23},{8,24},{9,... | collective-permute-start | bytes 3686408 | tf_op jit(solution)/shard_map/ppermute | solution.py:459
  272.4 65.4 %collective-permute-start.35 = (bf16[3,2,160,640]{3,2,1,0:T(8,128)(2,1)S(1)}, bf16[3,2,160,640]{3,2,1,0:T(8,128)(2,1)}, u32[]{:S(2)}, u32[]{:S(2)}) collective-permute-start(bf16[3,2,160,640]{3,2,1,0:T(8,128)(2,1)S(1)} %pad_maximum_fusion.9.refs_1_), channel_id=1, source_target_pairs={{0,8},{1,9},{2,10},{3,11},{4,12},{5,13},{6,14},{7,15},{8,0},{9,1},... | collective-permute-start | bytes 3686408 | tf_op jit(solution)/shard_map/ppermute | solution.py:459
  274.2 65.2 %collective-permute-start.36 = (bf16[3,2,160,640]{3,2,1,0:T(8,128)(2,1)S(1)}, bf16[3,2,160,640]{3,2,1,0:T(8,128)(2,1)}, u32[]{:S(2)}, u32[]{:S(2)}) collective-permute-start(bf16[3,2,160,640]{3,2,1,0:T(8,128)(2,1)S(1)} %pad_maximum_fusion.9.refs_1_), channel_id=1, source_target_pairs={{0,16},{1,17},{2,18},{3,19},{4,20},{5,21},{6,22},{7,23},{8,24},{9,... | collective-permute-start | bytes 3686408 | tf_op jit(solution)/shard_map/ppermute | solution.py:459
  283.0 56.5 %collective-permute-start.39 = (bf16[3,2,160,640]{3,2,1,0:T(8,128)(2,1)S(1)}, bf16[3,2,160,640]{3,2,1,0:T(8,128)(2,1)S(1)}, u32[]{:S(2)}, u32[]{:S(2)}) collective-permute-start(bf16[3,2,160,640]{3,2,1,0:T(8,128)(2,1)S(1)} %pad_maximum_fusion.9.refs_1_), channel_id=1, source_target_pairs={{0,4},{1,5},{2,6},{3,7},{4,0},{5,1},{6,2},{7,3},{8,12},{9,13},{10,... | collective-permute-start | bytes 3686408 | tf_op jit(solution)/shard_map/ppermute | solution.py:459
  363.3 58.2 %collective-permute-start.61 = (bf16[3,2,80,1280]{3,2,1,0:T(8,128)(2,1)S(1)}, bf16[3,2,80,1280]{3,2,1,0:T(8,128)(2,1)S(1)}, u32[]{:S(2)}, u32[]{:S(2)}) collective-permute-start(bf16[3,2,80,1280]{3,2,1,0:T(8,128)(2,1)S(1)} %pad_maximum_fusion.11.refs_1_), channel_id=1, source_target_pairs={{0,8},{1,9},{2,10},{3,11},{4,12},{5,13},{6,14},{7,15},{8,0},{9,1},... | collective-permute-start | bytes 3686408 | tf_op jit(solution)/shard_map/ppermute | solution.py:459
  364.1 60.2 %collective-permute-start.62 = (bf16[3,2,80,1280]{3,2,1,0:T(8,128)(2,1)S(1)}, bf16[3,2,80,1280]{3,2,1,0:T(8,128)(2,1)}, u32[]{:S(2)}, u32[]{:S(2)}) collective-permute-start(bf16[3,2,80,1280]{3,2,1,0:T(8,128)(2,1)S(1)} %pad_maximum_fusion.11.refs_1_), channel_id=1, source_target_pairs={{0,16},{1,17},{2,18},{3,19},{4,20},{5,21},{6,22},{7,23},{8,24},{9,... | collective-permute-start | bytes 3686408 | tf_op jit(solution)/shard_map/ppermute | solution.py:459
  381.2 49.6 %collective-permute-start.28 = (bf16[3,2,80,1280]{3,2,1,0:T(8,128)(2,1)}, bf16[3,2,80,1280]{3,2,1,0:T(8,128)(2,1)}, u32[]{:S(2)}, u32[]{:S(2)}) collective-permute-start(bf16[3,2,80,1280]{3,2,1,0:T(8,128)(2,1)} %collective-permute-done.23.refs_2_), channel_id=1, source_target_pairs={{0,4},{1,5},{2,6},{3,7},{4,0},{5,1},{6,2},{7,3},{8,12},{9,13},{10,... | collective-permute-start | bytes 3686408 | tf_op jit(solution)/shard_map/ppermute | solution.py:459
  424.2 420.2 %collective-permute-start.73 = (bf16[3,2,160,640]{3,2,1,0:T(8,128)(2,1)}, bf16[3,2,160,640]{3,2,1,0:T(8,128)(2,1)}, u32[]{:S(2)}, u32[]{:S(2)}) collective-permute-start(bf16[3,2,160,640]{3,2,1,0:T(8,128)(2,1)} %pad_maximum_fusion.12.refs_1_), channel_id=1, source_target_pairs={{0,8},{1,9},{2,10},{3,11},{4,12},{5,13},{6,14},{7,15},{8,0},{9,1},... | collective-permute-start | bytes 3686408 | tf_op jit(solution)/shard_map/ppermute | solution.py:459
  430.4 413.9 %collective-permute-start.50 = (bf16[3,2,80,640]{3,2,1,0:T(8,128)(2,1)}, bf16[3,2,80,640]{3,2,1,0:T(8,128)(2,1)S(1)}, u32[]{:S(2)}, u32[]{:S(2)}) collective-permute-start(bf16[3,2,80,640]{3,2,1,0:T(8,128)(2,1)} %slice.344), channel_id=1, source_target_pairs={{0,8},{1,9},{2,10},{3,11},{4,12},{5,13},{6,14},{7,15},{8,0},{9,1},... | collective-permute-start | bytes 1843208 | tf_op jit(solution)/shard_map/ppermute | solution.py:459
  430.9 423.3 %collective-permute-start.74 = (bf16[3,2,160,640]{3,2,1,0:T(8,128)(2,1)}, bf16[3,2,160,640]{3,2,1,0:T(8,128)(2,1)}, u32[]{:S(2)}, u32[]{:S(2)}) collective-permute-start(bf16[3,2,160,640]{3,2,1,0:T(8,128)(2,1)} %pad_maximum_fusion.12.refs_1_), channel_id=1, source_target_pairs={{0,16},{1,17},{2,18},{3,19},{4,20},{5,21},{6,22},{7,23},{8,24},{9,... | collective-permute-start | bytes 3686408 | tf_op jit(solution)/shard_map/ppermute | solution.py:459
  431.5 424.1 %collective-permute-start.40 = (bf16[3,2,160,640]{3,2,1,0:T(8,128)(2,1)}, bf16[3,2,160,640]{3,2,1,0:T(8,128)(2,1)}, u32[]{:S(2)}, u32[]{:S(2)}) collective-permute-start(bf16[3,2,160,640]{3,2,1,0:T(8,128)(2,1)} %collective-permute-done.35.refs_2_), channel_id=1, source_target_pairs={{0,4},{1,5},{2,6},{3,7},{4,0},{5,1},{6,2},{7,3},{8,12},{9,13},{10,... | collective-permute-start | bytes 3686408 | tf_op jit(solution)/shard_map/ppermute | solution.py:459
  442.5 413.5 %collective-permute-start.41 = (bf16[3,2,160,640]{3,2,1,0:T(8,128)(2,1)}, bf16[3,2,160,640]{3,2,1,0:T(8,128)(2,1)}, u32[]{:S(2)}, u32[]{:S(2)}) collective-permute-start(bf16[3,2,160,640]{3,2,1,0:T(8,128)(2,1)} %collective-permute-done.36.refs_3_), channel_id=1, source_target_pairs={{0,4},{1,5},{2,6},{3,7},{4,0},{5,1},{6,2},{7,3},{8,12},{9,13},{10,... | collective-permute-start | bytes 3686408 | tf_op jit(solution)/shard_map/ppermute | solution.py:459
  854.2 1221.5 %collective-permute-start.18 = (bf16[1280,512]{1,0:T(8,128)(2,1)}, bf16[1280,512]{1,0:T(8,128)(2,1)}, u32[]{:S(2)}, u32[]{:S(2)}) collective-permute-start(bf16[1280,512]{1,0:T(8,128)(2,1)} %fusion.72.v0), channel_id=1, source_target_pairs={{0,4},{1,5},{2,6},{3,7},{4,0},{5,1},{6,2},{7,3},{8,12},{9,13},{10,... | collective-permute-start | bytes 3932168 | tf_op jit(solution)/shard_map/ppermute | solution.py:459
  855.1 1221.1 %collective-permute-start.17 = (bf16[1280,512]{1,0:T(8,128)(2,1)S(1)}, bf16[1280,512]{1,0:T(8,128)(2,1)S(1)}, u32[]{:S(2)}, u32[]{:S(2)}) collective-permute-start(bf16[1280,512]{1,0:T(8,128)(2,1)S(1)} %convolution_convert_fusion.9.k0), channel_id=1, source_target_pairs={{0,4},{1,5},{2,6},{3,7},{4,0},{5,1},{6,2},{7,3},{8,12},{9,13},{10,... | collective-permute-start | bytes 3932168 | tf_op jit(solution)/shard_map/ppermute | solution.py:459
  855.5 821.1 %collective-permute-start.52 = (bf16[3,4,80,640]{3,2,1,0:T(8,128)(2,1)}, bf16[3,4,80,640]{3,2,1,0:T(8,128)(2,1)}, u32[]{:S(2)}, u32[]{:S(2)}) collective-permute-start(bf16[3,4,80,640]{3,2,1,0:T(8,128)(2,1)} %collective-permute-done.47.refs_5_), channel_id=1, source_target_pairs={{0,4},{1,5},{2,6},{3,7},{4,0},{5,1},{6,2},{7,3},{8,12},{9,13},{10,... | collective-permute-start | bytes 3686408 | tf_op jit(solution)/shard_map/ppermute | solution.py:459
  855.6 821.2 %collective-permute-start.53 = (bf16[3,4,80,640]{3,2,1,0:T(8,128)(2,1)}, bf16[3,4,80,640]{3,2,1,0:T(8,128)(2,1)}, u32[]{:S(2)}, u32[]{:S(2)}) collective-permute-start(bf16[3,4,80,640]{3,2,1,0:T(8,128)(2,1)} %collective-permute-done.48.refs_6_), channel_id=1, source_target_pairs={{0,4},{1,5},{2,6},{3,7},{4,0},{5,1},{6,2},{7,3},{8,12},{9,13},{10,... | collective-permute-start | bytes 3686408 | tf_op jit(solution)/shard_map/ppermute | solution.py:459
  863.8 812.4 %collective-permute-start.55 = (bf16[3,2,80,640]{3,2,1,0:T(8,128)(2,1)}, bf16[3,2,80,640]{3,2,1,0:T(8,128)(2,1)}, u32[]{:S(2)}, u32[]{:S(2)}) collective-permute-start(bf16[3,2,80,640]{3,2,1,0:T(8,128)(2,1)} %copy-done.127), channel_id=1, source_target_pairs={{0,4},{1,5},{2,6},{3,7},{4,0},{5,1},{6,2},{7,3},{8,12},{9,13},{10,... | collective-permute-start | bytes 1843208 | tf_op jit(solution)/shard_map/ppermute | solution.py:459
  1676.2 449.6 %collective-permute-start.65 = (bf16[3,2,80,1280]{3,2,1,0:T(8,128)(2,1)}, bf16[3,2,80,1280]{3,2,1,0:T(8,128)(2,1)}, u32[]{:S(2)}, u32[]{:S(2)}) collective-permute-start(bf16[3,2,80,1280]{3,2,1,0:T(8,128)(2,1)} %copy-done.54), channel_id=1, source_target_pairs={{0,4},{1,5},{2,6},{3,7},{4,0},{5,1},{6,2},{7,3},{8,12},{9,13},{10,... | collective-permute-start | bytes 3686408 | tf_op jit(solution)/shard_map/ppermute | solution.py:459
  1676.6 451.5 %collective-permute-start.77 = (bf16[3,2,160,640]{3,2,1,0:T(8,128)(2,1)}, bf16[3,2,160,640]{3,2,1,0:T(8,128)(2,1)}, u32[]{:S(2)}, u32[]{:S(2)}) collective-permute-start(bf16[3,2,160,640]{3,2,1,0:T(8,128)(2,1)} %pad_maximum_fusion.12.refs_1_), channel_id=1, source_target_pairs={{0,4},{1,5},{2,6},{3,7},{4,0},{5,1},{6,2},{7,3},{8,12},{9,13},{10,... | collective-permute-start | bytes 3686408 | tf_op jit(solution)/shard_map/ppermute | solution.py:459
  1676.8 452.9 %collective-permute-start.63 = (bf16[3,1,80,1280]{3,2,1,0:T(8,128)(2,1)}, bf16[3,1,80,1280]{3,2,1,0:T(8,128)(2,1)}, u32[]{:S(2)}, u32[]{:S(2)}) collective-permute-start(bf16[3,1,80,1280]{3,2,1,0:T(8,128)(2,1)} %slice.347), channel_id=1, source_target_pairs={{0,16},{1,17},{2,18},{3,19},{4,20},{5,21},{6,22},{7,23},{8,24},{9,... | collective-permute-start | bytes 1843208 | tf_op jit(solution)/shard_map/ppermute | solution.py:459
  2075.7 54.7 %collective-permute-start.64 = (bf16[3,1,80,1280]{3,2,1,0:T(8,128)(2,1)}, bf16[3,1,80,1280]{3,2,1,0:T(8,128)(2,1)}, u32[]{:S(2)}, u32[]{:S(2)}) collective-permute-start(bf16[3,1,80,1280]{3,2,1,0:T(8,128)(2,1)} %slice.348), channel_id=1, source_target_pairs={{0,8},{1,9},{2,10},{3,11},{4,12},{5,13},{6,14},{7,15},{8,0},{9,1},... | collective-permute-start | bytes 1843208 | tf_op jit(solution)/shard_map/ppermute | solution.py:459
  2076.2 54.6 %collective-permute-start.75 = (bf16[3,1,160,640]{3,2,1,0:T(8,128)(2,1)}, bf16[3,1,160,640]{3,2,1,0:T(8,128)(2,1)}, u32[]{:S(2)}, u32[]{:S(2)}) collective-permute-start(bf16[3,1,160,640]{3,2,1,0:T(8,128)(2,1)} %slice.349), channel_id=1, source_target_pairs={{0,16},{1,17},{2,18},{3,19},{4,20},{5,21},{6,22},{7,23},{8,24},{9,... | collective-permute-start | bytes 1843208 | tf_op jit(solution)/shard_map/ppermute | solution.py:459
  2163.6 439.6 %collective-permute-start.78 = (bf16[3,2,160,640]{3,2,1,0:T(8,128)(2,1)}, bf16[3,2,160,640]{3,2,1,0:T(8,128)(2,1)}, u32[]{:S(2)}, u32[]{:S(2)}) collective-permute-start(bf16[3,2,160,640]{3,2,1,0:T(8,128)(2,1)} %collective-permute-done.73.refs_2_), channel_id=1, source_target_pairs={{0,4},{1,5},{2,6},{3,7},{4,0},{5,1},{6,2},{7,3},{8,12},{9,13},{10,... | collective-permute-start | bytes 3686408 | tf_op jit(solution)/shard_map/ppermute | solution.py:459
  2163.7 439.6 %collective-permute-start.79 = (bf16[3,2,160,640]{3,2,1,0:T(8,128)(2,1)}, bf16[3,2,160,640]{3,2,1,0:T(8,128)(2,1)}, u32[]{:S(2)}, u32[]{:S(2)}) collective-permute-start(bf16[3,2,160,640]{3,2,1,0:T(8,128)(2,1)} %collective-permute-done.74.refs_3_), channel_id=1, source_target_pairs={{0,4},{1,5},{2,6},{3,7},{4,0},{5,1},{6,2},{7,3},{8,12},{9,13},{10,... | collective-permute-start | bytes 3686408 | tf_op jit(solution)/shard_map/ppermute | solution.py:459
  2164.2 837.3 %collective-permute-start.57 = (bf16[1280,512]{1,0:T(8,128)(2,1)}, bf16[1280,512]{1,0:T(8,128)(2,1)}, u32[]{:S(2)}, u32[]{:S(2)}) collective-permute-start(bf16[1280,512]{1,0:T(8,128)(2,1)} %fusion.73.v0), channel_id=1, source_target_pairs={{0,4},{1,5},{2,6},{3,7},{4,0},{5,1},{6,2},{7,3},{8,12},{9,13},{10,... | collective-permute-start | bytes 3932168 | tf_op jit(solution)/shard_map/ppermute | solution.py:459
  2164.2 837.2 %collective-permute-start.56 = (bf16[1280,512]{1,0:T(8,128)(2,1)S(1)}, bf16[1280,512]{1,0:T(8,128)(2,1)S(1)}, u32[]{:S(2)}, u32[]{:S(2)}) collective-permute-start(bf16[1280,512]{1,0:T(8,128)(2,1)S(1)} %convolution_convert_fusion.8.k0), channel_id=1, source_target_pairs={{0,4},{1,5},{2,6},{3,7},{4,0},{5,1},{6,2},{7,3},{8,12},{9,13},{10,... | collective-permute-start | bytes 3932168 | tf_op jit(solution)/shard_map/ppermute | solution.py:459
  2164.7 438.1 %collective-permute-start.81 = (bf16[3,1,160,640]{3,2,1,0:T(8,128)(2,1)}, bf16[3,1,160,640]{3,2,1,0:T(8,128)(2,1)}, u32[]{:S(2)}, u32[]{:S(2)}) collective-permute-start(bf16[3,1,160,640]{3,2,1,0:T(8,128)(2,1)} %collective-permute-done.76.refs_5_), channel_id=1, source_target_pairs={{0,4},{1,5},{2,6},{3,7},{4,0},{5,1},{6,2},{7,3},{8,12},{9,13},{10,... | collective-permute-start | bytes 1843208 | tf_op jit(solution)/shard_map/ppermute | solution.py:459
  2602.8 696.7 %collective-permute-start.107 = (bf16[512,1280]{1,0:T(8,128)(2,1)}, bf16[512,1280]{1,0:T(8,128)(2,1)}, u32[]{:S(2)}, u32[]{:S(2)}) collective-permute-start(bf16[512,1280]{1,0:T(8,128)(2,1)} %copy-done.101), channel_id=1, source_target_pairs={{0,4},{1,5},{2,6},{3,7},{4,0},{5,1},{6,2},{7,3},{8,12},{9,13},{10,... | collective-permute-start | bytes 3932168 | tf_op jit(solution)/shard_map/ppermute | solution.py:459
  3023.1 221.7 %collective-permute-start.135 = (bf16[1280,512]{1,0:T(8,128)(2,1)}, bf16[1280,512]{1,0:T(8,128)(2,1)}, u32[]{:S(2)}, u32[]{:S(2)}) collective-permute-start(bf16[1280,512]{1,0:T(8,128)(2,1)} %get-tuple-element.55), channel_id=1, source_target_pairs={{0,4},{1,5},{2,6},{3,7},{4,0},{5,1},{6,2},{7,3},{8,12},{9,13},{10,... | collective-permute-start | bytes 3932168 | tf_op jit(solution)/shard_map/ppermute | solution.py:459
  3112.6 80.4 %collective-permute-start.86 = (bf16[1280,512]{1,0:T(8,128)(2,1)}, bf16[1280,512]{1,0:T(8,128)(2,1)}, u32[]{:S(2)}, u32[]{:S(2)}) collective-permute-start(bf16[1280,512]{1,0:T(8,128)(2,1)} %get-tuple-element.62), channel_id=1, source_target_pairs={{0,4},{1,5},{2,6},{3,7},{4,0},{5,1},{6,2},{7,3},{8,12},{9,13},{10,... | collective-permute-start | bytes 3932168 | tf_op jit(solution)/shard_map/ppermute | solution.py:459
  3189.9 54.8 %collective-permute-start.136 = (bf16[512,640]{1,0:T(8,128)(2,1)}, bf16[512,640]{1,0:T(8,128)(2,1)}, u32[]{:S(2)}, u32[]{:S(2)}) collective-permute-start(bf16[512,640]{1,0:T(8,128)(2,1)} %get-tuple-element.211), channel_id=1, source_target_pairs={{0,4},{1,5},{2,6},{3,7},{4,0},{5,1},{6,2},{7,3},{8,12},{9,13},{10,... | collective-permute-start | bytes 1966088 | tf_op jit(solution)/shard_map/ppermute | solution.py:459
  3193.0 107.0 %collective-permute-start.108 = (bf16[640,512]{1,0:T(8,128)(2,1)}, bf16[640,512]{1,0:T(8,128)(2,1)}, u32[]{:S(2)}, u32[]{:S(2)}) collective-permute-start(bf16[640,512]{1,0:T(8,128)(2,1)} %get-tuple-element.219), channel_id=1, source_target_pairs={{0,4},{1,5},{2,6},{3,7},{4,0},{5,1},{6,2},{7,3},{8,12},{9,13},{10,... | collective-permute-start | bytes 1966088 | tf_op jit(solution)/shard_map/ppermute | solution.py:459
  3299.4 101.9 %collective-permute-start.188 = (bf16[512,1280]{1,0:T(8,128)(2,1)}, bf16[512,1280]{1,0:T(8,128)(2,1)}, u32[]{:S(2)}, u32[]{:S(2)}) collective-permute-start(bf16[512,1280]{1,0:T(8,128)(2,1)} %get-tuple-element.128), channel_id=1, source_target_pairs={{0,4},{1,5},{2,6},{3,7},{4,0},{5,1},{6,2},{7,3},{8,12},{9,13},{10,... | collective-permute-start | bytes 3932168 | tf_op jit(solution)/shard_map/ppermute | solution.py:459
  3300.0 244.8 %collective-permute-start.92 = (bf16[512,1280]{1,0:T(8,128)(2,1)}, bf16[512,1280]{1,0:T(8,128)(2,1)}, u32[]{:S(2)}, u32[]{:S(2)}) collective-permute-start(bf16[512,1280]{1,0:T(8,128)(2,1)} %fusion.76), channel_id=1, source_target_pairs={{0,4},{1,5},{2,6},{3,7},{4,0},{5,1},{6,2},{7,3},{8,12},{9,13},{10,... | collective-permute-start | bytes 3932168 | tf_op jit(solution)/shard_map/ppermute | solution.py:459
  3366.0 50.1 %collective-permute-start.161 = (bf16[512,1280]{1,0:T(8,128)(2,1)}, bf16[512,1280]{1,0:T(8,128)(2,1)}, u32[]{:S(2)}, u32[]{:S(2)}) collective-permute-start(bf16[512,1280]{1,0:T(8,128)(2,1)} %add_convert_fusion.4), channel_id=1, source_target_pairs={{0,4},{1,5},{2,6},{3,7},{4,0},{5,1},{6,2},{7,3},{8,12},{9,13},{10,... | collective-permute-start | bytes 3932168 | tf_op jit(solution)/shard_map/ppermute | solution.py:459
  3401.3 140.7 %collective-permute-start.113 = (bf16[4,2,80,896]{3,2,0,1:T(8,128)(2,1)}, bf16[4,2,80,896]{3,2,0,1:T(8,128)(2,1)}, u32[]{:S(2)}, u32[]{:S(2)}) collective-permute-start(bf16[4,2,80,896]{3,2,0,1:T(8,128)(2,1)} %bitcast.522), channel_id=1, source_target_pairs={{0,16},{1,17},{2,18},{3,19},{4,20},{5,21},{6,22},{7,23},{8,24},{9,... | collective-permute-start | bytes 3440648 | tf_op jit(solution)/shard_map/ppermute | solution.py:459
  3416.1 101.1 %collective-permute-start.125 = (bf16[4,80,384]{2,1,0:T(8,128)(2,1)}, bf16[4,80,384]{2,1,0:T(8,128)(2,1)}, u32[]{:S(2)}, u32[]{:S(2)}) collective-permute-start(bf16[4,80,384]{2,1,0:T(8,128)(2,1)} %dynamic-slice_bitcast_fusion.27), channel_id=1, source_target_pairs={{0,16},{1,17},{2,18},{3,19},{4,20},{5,21},{6,22},{7,23},{8,24},{9,... | collective-permute-start | bytes 737288 | tf_op jit(solution)/shard_map/ppermute | solution.py:459
  3542.0 83.7 %collective-permute-start.148 = (bf16[512,1280]{1,0:T(8,128)(2,1)}, bf16[512,1280]{1,0:T(8,128)(2,1)}, u32[]{:S(2)}, u32[]{:S(2)}) collective-permute-start(bf16[512,1280]{1,0:T(8,128)(2,1)} %add_convert_fusion.6), channel_id=1, source_target_pairs={{0,4},{1,5},{2,6},{3,7},{4,0},{5,1},{6,2},{7,3},{8,12},{9,13},{10,... | collective-permute-start | bytes 3932168 | tf_op jit(solution)/shard_map/ppermute | solution.py:459
  3544.8 80.9 %collective-permute-start.149 = (bf16[512,2560]{1,0:T(8,128)(2,1)}, bf16[512,2560]{1,0:T(8,128)(2,1)}, u32[]{:S(2)}, u32[]{:S(2)}) collective-permute-start(bf16[512,2560]{1,0:T(8,128)(2,1)} %get-tuple-element.155), channel_id=1, source_target_pairs={{0,4},{1,5},{2,6},{3,7},{4,0},{5,1},{6,2},{7,3},{8,12},{9,13},{10,... | collective-permute-start | bytes 7864328 | tf_op jit(solution)/shard_map/ppermute | solution.py:459
  3563.9 104.8 %collective-permute-start.178 = (bf16[4,2,160,640]{3,2,1,0:T(8,128)(2,1)}, bf16[4,2,160,640]{3,2,1,0:T(8,128)(2,1)}, u32[]{:S(2)}, u32[]{:S(2)}) collective-permute-start(bf16[4,2,160,640]{3,2,1,0:T(8,128)(2,1)} %dynamic-slice_bitcast_fusion.1), channel_id=1, source_target_pairs={{0,16},{1,17},{2,18},{3,19},{4,20},{5,21},{6,22},{7,23},{8,24},{9,... | collective-permute-start | bytes 4915208 | tf_op jit(solution)/shard_map/ppermute | solution.py:459
  3578.8 92.9 %collective-permute-start.176 = (bf16[4,2,160,640]{3,2,0,1:T(8,128)(2,1)}, bf16[4,2,160,640]{3,2,0,1:T(8,128)(2,1)}, u32[]{:S(2)}, u32[]{:S(2)}) collective-permute-start(bf16[4,2,160,640]{3,2,0,1:T(8,128)(2,1)} %bitcast.517), channel_id=1, source_target_pairs={{0,8},{1,9},{2,10},{3,11},{4,12},{5,13},{6,14},{7,15},{8,0},{9,1},... | collective-permute-start | bytes 4915208 | tf_op jit(solution)/shard_map/ppermute | solution.py:459
  3668.1 49.0 %collective-permute-start.165 = (bf16[4,2,80,1280]{3,2,1,0:T(8,128)(2,1)S(1)}, bf16[4,2,80,1280]{3,2,1,0:T(8,128)(2,1)S(1)}, u32[]{:S(2)}, u32[]{:S(2)}) collective-permute-start(bf16[4,2,80,1280]{3,2,1,0:T(8,128)(2,1)S(1)} %copy-done.96), channel_id=1, source_target_pairs={{0,16},{1,17},{2,18},{3,19},{4,20},{5,21},{6,22},{7,23},{8,24},{9,... | collective-permute-start | bytes 4915208 | tf_op jit(solution)/shard_map/ppermute | solution.py:459
  3668.8 65.3 %collective-permute-start.163 = (bf16[4,2,80,1280]{3,2,0,1:T(8,128)(2,1)S(1)}, bf16[4,2,80,1280]{3,2,0,1:T(8,128)(2,1)S(1)}, u32[]{:S(2)}, u32[]{:S(2)}) collective-permute-start(bf16[4,2,80,1280]{3,2,0,1:T(8,128)(2,1)S(1)} %bitcast.566), channel_id=1, source_target_pairs={{0,8},{1,9},{2,10},{3,11},{4,12},{5,13},{6,14},{7,15},{8,0},{9,1},... | collective-permute-start | bytes 4915208 | tf_op jit(solution)/shard_map/ppermute | solution.py:459
  3671.8 69.9 %collective-permute-start.98 = (bf16[4,2,80,896]{3,2,0,1:T(8,128)(2,1)S(1)}, bf16[4,2,80,896]{3,2,0,1:T(8,128)(2,1)S(1)}, u32[]{:S(2)}, u32[]{:S(2)}) collective-permute-start(bf16[4,2,80,896]{3,2,0,1:T(8,128)(2,1)S(1)} %bitcast.580), channel_id=1, source_target_pairs={{0,16},{1,17},{2,18},{3,19},{4,20},{5,21},{6,22},{7,23},{8,24},{9,... | collective-permute-start | bytes 3440648 | tf_op jit(solution)/shard_map/ppermute | solution.py:459
  3682.0 131.5 %collective-permute-start.96 = (bf16[4,2,80,1024]{3,2,0,1:T(8,128)(2,1)S(1)}, bf16[4,2,80,1024]{3,2,0,1:T(8,128)(2,1)S(1)}, u32[]{:S(2)}, u32[]{:S(2)}) collective-permute-start(bf16[4,2,80,1024]{3,2,0,1:T(8,128)(2,1)S(1)} %bitcast.575), channel_id=1, source_target_pairs={{0,8},{1,9},{2,10},{3,11},{4,12},{5,13},{6,14},{7,15},{8,0},{9,1},... | collective-permute-start | bytes 3932168 | tf_op jit(solution)/shard_map/ppermute | solution.py:459
  3699.0 316.6 %collective-permute-start.152 = (bf16[4,2,80,1280]{3,2,1,0:T(8,128)(2,1)S(1)}, bf16[4,2,80,1280]{3,2,1,0:T(8,128)(2,1)S(1)}, u32[]{:S(2)}, u32[]{:S(2)}) collective-permute-start(bf16[4,2,80,1280]{3,2,1,0:T(8,128)(2,1)S(1)} %dynamic-slice_bitcast_fusion.3), channel_id=1, source_target_pairs={{0,16},{1,17},{2,18},{3,19},{4,20},{5,21},{6,22},{7,23},{8,24},{9,... | collective-permute-start | bytes 4915208 | tf_op jit(solution)/shard_map/ppermute | solution.py:459
  3717.1 300.3 %collective-permute-start.150 = (bf16[4,2,80,1280]{3,2,0,1:T(8,128)(2,1)S(1)}, bf16[4,2,80,1280]{3,2,0,1:T(8,128)(2,1)S(1)}, u32[]{:S(2)}, u32[]{:S(2)}) collective-permute-start(bf16[4,2,80,1280]{3,2,0,1:T(8,128)(2,1)S(1)} %bitcast.567), channel_id=1, source_target_pairs={{0,8},{1,9},{2,10},{3,11},{4,12},{5,13},{6,14},{7,15},{8,0},{9,1},... | collective-permute-start | bytes 4915208 | tf_op jit(solution)/shard_map/ppermute | solution.py:459
  3734.1 69.8 %collective-permute-start.118 = (bf16[80,1920]{1,0:T(8,128)(2,1)S(1)}, bf16[80,1920]{1,0:T(8,128)(2,1)S(1)}, u32[]{:S(2)}, u32[]{:S(2)}) collective-permute-start(bf16[80,1920]{1,0:T(8,128)(2,1)S(1)} %get-tuple-element.118), channel_id=1, source_target_pairs={{0,8},{1,9},{2,10},{3,11},{4,12},{5,13},{6,14},{7,15},{8,0},{9,1},... | collective-permute-start | bytes 921608 | tf_op jit(solution)/shard_map/ppermute | solution.py:459
  3741.7 63.1 %collective-permute-start.119 = (bf16[80,1920]{1,0:T(8,128)(2,1)S(1)}, bf16[80,1920]{1,0:T(8,128)(2,1)S(1)}, u32[]{:S(2)}, u32[]{:S(2)}) collective-permute-start(bf16[80,1920]{1,0:T(8,128)(2,1)S(1)} %get-tuple-element.118), channel_id=1, source_target_pairs={{0,16},{1,17},{2,18},{3,19},{4,20},{5,21},{6,22},{7,23},{8,24},{9,... | collective-permute-start | bytes 921608 | tf_op jit(solution)/shard_map/ppermute | solution.py:459
  4006.2 53.1 %collective-permute-start.183 = (bf16[160,1280]{1,0:T(8,128)(2,1)}, bf16[160,1280]{1,0:T(8,128)(2,1)}, u32[]{:S(2)}, u32[]{:S(2)}) collective-permute-start(bf16[160,1280]{1,0:T(8,128)(2,1)} %get-tuple-element.104), channel_id=1, source_target_pairs={{0,8},{1,9},{2,10},{3,11},{4,12},{5,13},{6,14},{7,15},{8,0},{9,1},... | collective-permute-start | bytes 1228808 | tf_op jit(solution)/shard_map/ppermute | solution.py:459
  4051.3 53.6 %collective-permute-start.197 = (bf16[160,1280]{1,0:T(8,128)(2,1)S(1)}, bf16[160,1280]{1,0:T(8,128)(2,1)S(1)}, u32[]{:S(2)}, u32[]{:S(2)}) collective-permute-start(bf16[160,1280]{1,0:T(8,128)(2,1)S(1)} %copy-done.94), channel_id=1, source_target_pairs={{0,16},{1,17},{2,18},{3,19},{4,20},{5,21},{6,22},{7,23},{8,24},{9,... | collective-permute-start | bytes 1228808 | tf_op jit(solution)/shard_map/ppermute | solution.py:459
  4097.7 53.2 %collective-permute-start.106 = (bf16[4,80,1920]{2,1,0:T(8,128)(2,1)S(1)}, bf16[4,80,1920]{2,1,0:T(8,128)(2,1)S(1)}, u32[]{:S(2)}, u32[]{:S(2)}) collective-permute-start(bf16[4,80,1920]{2,1,0:T(8,128)(2,1)S(1)} %pad_maximum_fusion.13), channel_id=1, source_target_pairs={{0,4},{1,5},{2,6},{3,7},{4,0},{5,1},{6,2},{7,3},{8,12},{9,13},{10,... | collective-permute-start | bytes 3686408 | tf_op jit(solution)/shard_map/ppermute | solution.py:459
  4104.9 90.3 %collective-permute-start.186 = (bf16[4,160,1280]{2,1,0:T(8,128)(2,1)}, bf16[4,160,1280]{2,1,0:T(8,128)(2,1)}, u32[]{:S(2)}, u32[]{:S(2)}) collective-permute-start(bf16[4,160,1280]{2,1,0:T(8,128)(2,1)} %pad_maximum_fusion.2), channel_id=1, source_target_pairs={{0,4},{1,5},{2,6},{3,7},{4,0},{5,1},{6,2},{7,3},{8,12},{9,13},{10,... | collective-permute-start | bytes 4915208 | tf_op jit(solution)/shard_map/ppermute | solution.py:459
  4120.7 82.5 %collective-permute-start.199 = (bf16[4,160,1280]{2,1,0:T(8,128)(2,1)}, bf16[4,160,1280]{2,1,0:T(8,128)(2,1)}, u32[]{:S(2)}, u32[]{:S(2)}) collective-permute-start(bf16[4,160,1280]{2,1,0:T(8,128)(2,1)} %pad_maximum_fusion.3), channel_id=1, source_target_pairs={{0,4},{1,5},{2,6},{3,7},{4,0},{5,1},{6,2},{7,3},{8,12},{9,13},{10,... | collective-permute-start | bytes 4915208 | tf_op jit(solution)/shard_map/ppermute | solution.py:459
  4189.9 53.4 %collective-permute-start.160 = (bf16[4,80,2560]{2,1,0:T(8,128)(2,1)}, bf16[4,80,2560]{2,1,0:T(8,128)(2,1)}, u32[]{:S(2)}, u32[]{:S(2)}) collective-permute-start(bf16[4,80,2560]{2,1,0:T(8,128)(2,1)} %pad_maximum_fusion), channel_id=1, source_target_pairs={{0,4},{1,5},{2,6},{3,7},{4,0},{5,1},{6,2},{7,3},{8,12},{9,13},{10,... | collective-permute-start | bytes 4915208 | tf_op jit(solution)/shard_map/ppermute | solution.py:459
  (339 other events, 13579.9 us)
Sparse Core Ops, SparseCore 0:
  3393.0 121.3 all-reduce.1
